TPU v7x, 512 devices: a whole 4x4x16 slice. The times are simulated.
512 devices in a mesh: region: 32 (over z, core), group: 16 (over x, y).
Axes of the slice: x: 4, y: 4, z: 16, core: 2. Of those that a mesh axis runs over, the one named last changes fastest.
Arguments:
- features: bfloat16 [196608, 2048], P(('region', 'group')), may hold values from -1.5 to 1.5
- memory: bfloat16 [65536, 2048], P(('region', 'group')), may hold values from -1 to 1
- requests: int32 [512, 8], P(('region', 'group')), may hold values from 0 to 15, as said below
- owners: int32 [32, 16], P('region'), may hold values from 0 to 15, as said below
- labels: int32 [512, 384], P(('region', 'group')), may hold values from 0 to 4095, as said below
Outputs:
- feat_grad: bfloat16 [196608, 2048], P(('region', 'group'))
- new_memory: bfloat16 [65536, 2048], P(('region', 'group'))
Inputs may be any that keep to these rules, and one draw needn't show every extreme that they name: `owners`: each row of a region is a permutation. `requests`: the 8 numbers of a device are distinct blocks of its region. At most 24 crops of one device carry labels of one region, and every device reaches that bound for some region.
All inputs are finite; a program needn't handle non-finite values.
Results may differ from a plain program's by a relative error of at most 0.006.
Values may be sent and summed in bfloat16 or wider, within the bound.
A program may use at most 64 MiB of HBM per device.

v0:
```python
import jax
import jax.numpy as jnp
from jax import lax
from jax.sharding import PartitionSpec as P

D = 2048


exponent_sharpness = 0.05
smoothing = 0.1
momentum_keep = 0.2


def on_device(features, memory, requests, owners, labels):
    group_count = lax.axis_size("group")
    region_count = lax.axis_size("region")
    block_rows = memory.shape[0]
    feat_width = memory.shape[1]
    crop_count = features.shape[0]
    wanted_owner = jnp.take(owners[0], requests[0], axis=0)
    arrived = lax.all_gather(memory, "group", axis=0, tiled=True).reshape(
        group_count, block_rows, feat_width
    )
    reciprocal_memory_slices = jnp.take(arrived, wanted_owner, axis=0).reshape(-1, feat_width)
    cand_count = reciprocal_memory_slices.shape[0]
    cosine_affinities = (
        lax.dot_general(
            features,
            reciprocal_memory_slices,
            (((1,), (1,)), ((), ())),
            preferred_element_type=jnp.float32,
        )
        / exponent_sharpness
    )
    shifted = cosine_affinities - jnp.max(cosine_affinities, axis=1, keepdims=True)
    expo = jnp.exp(shifted)
    normalized_likelihoods = expo / jnp.sum(expo, axis=1, keepdims=True)
    column = jnp.arange(cand_count, dtype=jnp.int32)
    smoothed_identity_weights = (
        jnp.where(column < block_rows, (1.0 - smoothing) / block_rows, 0.0) + smoothing / cand_count
    ).astype(jnp.float32)
    pre_normalized_derivative = (
        (normalized_likelihoods - smoothed_identity_weights[None, :]) / exponent_sharpness
    ).astype(jnp.bfloat16)
    feat_grad = jnp.dot(
        pre_normalized_derivative, reciprocal_memory_slices, preferred_element_type=jnp.float32
    ).astype(jnp.bfloat16)
    capacity = max(2, 2 * crop_count // region_count)
    label_row = labels[0]
    label_region = label_row // block_rows
    label_offset = label_row % block_rows
    region_onehot = (
        label_region[:, None] == jnp.arange(region_count, dtype=jnp.int32)[None, :]
    ).astype(jnp.int32)
    earlier = jnp.sum((jnp.cumsum(region_onehot, axis=0) - region_onehot) * region_onehot, axis=1)
    slot_of = label_region * capacity + earlier
    slot_match = jnp.arange(region_count * capacity, dtype=jnp.int32)[:, None] == slot_of[None, :]
    packed = jnp.dot(
        slot_match.astype(jnp.bfloat16), features, preferred_element_type=jnp.float32
    ).astype(jnp.bfloat16)
    packed = packed.reshape(region_count, capacity, feat_width)
    slot_offsets = (
        jnp.sum(jnp.where(slot_match, label_offset[None, :] + 1, 0), axis=1) - 1
    ).reshape(region_count, capacity)
    received, received_offsets = (
        lax.all_to_all(packed, "region", split_axis=0, concat_axis=0, tiled=True),
        lax.all_to_all(slot_offsets, "region", split_axis=0, concat_axis=0, tiled=True),
    )
    received_rows = received.reshape(-1, feat_width)
    row_match = (
        jnp.arange(block_rows, dtype=jnp.int32)[:, None] == received_offsets.reshape(-1)[None, :]
    )
    sums = jnp.dot(
        row_match.astype(jnp.bfloat16), received_rows, preferred_element_type=jnp.float32
    )
    counts = jnp.sum(row_match.astype(jnp.float32), axis=1)
    old_rows = memory.astype(jnp.float32)
    averaged = sums / jnp.maximum(counts, 1.0)[:, None]
    mixed = jnp.where(
        counts[:, None] > 0, momentum_keep * old_rows + (1.0 - momentum_keep) * averaged, old_rows
    )
    scale = lax.rsqrt(jnp.mean(mixed * mixed, axis=1, keepdims=True) + 1e-06) * D ** (-0.5)
    new_memory = (mixed * scale).astype(jnp.bfloat16)
    return (feat_grad, new_memory)


def solution(mesh):
    placed = (
        P(("region", "group"), None),
        P(("region", "group"), None),
        P(("region", "group"), None),
        P("region", None),
        P(("region", "group"), None),
    )
    return jax.shard_map(
        on_device,
        mesh=mesh,
        in_specs=placed,
        out_specs=(P(("region", "group"), None), P(("region", "group"), None)),
        check_vma=False,
    )
```

profile of v0, /device:TPU:1, one launch (start us, length us, event | category | flops | bytes accessed | tf_op | source)
XLA Modules:
  0.0 212.2 jit_solution(8317848267126924623)
XLA Ops:
  7.2 0.7 all-gather.2.cloned.1.call-update
  7.9 0.7 reduce.2
  8.6 0.9 reduce-window.6
  9.5 0.2 slice_reduce_fusion
  9.8 0.1 fusion.12
  9.9 0.7 fusion.20
  10.6 0.2 select_reduce_fusion
  10.8 0.7 sub.45
  11.5 16.7 %all-to-all-start = ((s32[32,1,24]{2,1,0:T(1,128)}), s32[32,1,24]{2,1,0:T(1,128)S(1)}, u32[]{:S(2)}, u32[]{:S(2)}) async-start(s32[32,1,24]{2,1,0:T(1,128)} %bitcast.10), calls=%async_computation | async-start | bytes 32768 | tf_op jit(solution)/shard_map/all_to_all | solution.py:67
  28.3 3.5 %convolution_convert_fusion = bf16[768,2048]{1,0:T(8,128)(2,1)} fusion(bf16[384,2048]{1,0:T(8,128)(2,1)S(1)} %copy-done, s32[384]{0:T(512)S(1)} %get-tuple-element.3), kind=kOutput, calls=%fused_computation.3 | convolution fusion | flops 1209827328 | bytes 4720128 | tf_op jit(solution)/shard_map/dot_general | solution.py:58
  31.8 8.2 %all-to-all-done = s32[32,1,24]{2,1,0:T(1,128)S(1)} async-done(((s32[32,1,24]{2,1,0:T(1,128)}), s32[32,1,24]{2,1,0:T(1,128)S(1)}, u32[]{:S(2)}, u32[]{:S(2)}) %all-to-all-start) | async-done | bytes 3104 | tf_op jit(solution)/shard_map/all_to_all | solution.py:67
  40.0 5.5 %all-to-all-start.1 = ((bf16[32,24,2048]{2,1,0:T(8,128)(2,1)}), bf16[32,24,2048]{2,1,0:T(8,128)(2,1)}, u32[]{:S(2)}, u32[]{:S(2)}) async-start(bf16[32,24,2048]{2,1,0:T(8,128)(2,1)} %bitcast.69), calls=%async_computation.1 | async-start | bytes 6291456 | tf_op jit(solution)/shard_map/all_to_all | solution.py:66
  45.5 0.6 gather_fusion
  46.3 0.5 broadcast.314
  46.8 0.7 reduce.13
  47.6 0.1 convert_reduce_fusion
  47.7 139.2 %all-to-all-done.1 = bf16[32,24,2048]{2,1,0:T(8,128)(2,1)} async-done(((bf16[32,24,2048]{2,1,0:T(8,128)(2,1)}), bf16[32,24,2048]{2,1,0:T(8,128)(2,1)}, u32[]{:S(2)}, u32[]{:S(2)}) %all-to-all-start.1) | async-done | bytes 3145760 | tf_op jit(solution)/shard_map/all_to_all | solution.py:66
  186.9 2.8 %multiply_reduce_fusion = (f32[128]{0:T(128)S(1)}, f32[128,2048]{1,0:T(8,128)S(1)}) fusion(f32[128]{0:T(128)S(1)} %broadcast_maximum_fusion, bf16[768,2048]{1,0:T(8,128)(2,1)} %bitcast.12, s32[768]{0:T(1024)S(1)} %eq.64, bf16[128,2048]{1,0:T(8,128)(2,1)S(1)} %copy-done.2, pred[128]{0:T(512)(128)(4,1)S(1)} %broadcast_compare_fusion), kind=kOutput, calls=%fused_computation.17 | convolution fusion | flops 404848512 | bytes 4722816 | tf_op jit(solution)/shard_map/dot_general | solution.py:73
  189.8 0.9 multiply_convert_fusion.1
  190.7 6.2 %gather_fusion.1 = bf16[8,128,2048]{2,1,0:T(8,128)(2,1)} fusion(bf16[16,128,2048]{2,1,0:T(8,128)(2,1)} %bitcast.70, s32[1024]{0:T(1024)S(1)} %pad_clamp_fusion), kind=kCustom, calls=%fused_computation.1 | custom fusion | bytes 8388640 | tf_op jit(solution)/shard_map/jit(_take)/gather | solution.py:24
  196.9 2.6 %bitcast_select_fusion = bf16[1024,2048]{1,0:T(8,128)(2,1)S(1)} fusion(bf16[8,128,2048]{2,1,0:T(8,128)(2,1)} %gather_fusion.1, pred[1024]{0:T(1024)(128)(4,1)S(1)} %broadcast_bitcast_fusion), kind=kLoop, calls=%fused_computation.2 | loop fusion | flops 2097152 | bytes 8389632 | tf_op jit(solution)/shard_map/jit(_take)/select_n | solution.py:24
  199.5 2.4 %fusion.24 = (f32[384]{0:T(512)S(1)}, f32[1024,384]{1,0:T(8,128)S(1)}) fusion(bf16[1024,2048]{1,0:T(8,128)(2,1)S(1)} %bitcast_select_fusion, bf16[384,2048]{1,0:T(8,128)(2,1)S(1)} %copy-done), kind=kOutput, calls=%fused_computation.78 | convolution fusion | flops 1611398784 | bytes 7341568 | tf_op jit(solution)/shard_map/dot_general | solution.py:27
  201.9 0.3 fusion.3
  202.2 3.2 %convolution_convert_fusion.1 = bf16[384,2048]{1,0:T(8,128)(2,1)} fusion(bf16[1024,2048]{1,0:T(8,128)(2,1)S(1)} %bitcast_select_fusion, f32[1024,384]{1,0:T(8,128)S(1)} %get-tuple-element.5, f32[1024]{0:T(1024)S(1)} %select_add_fusion, f32[384]{0:T(512)S(1)} %fusion.3, f32[384]{0:T(512)S(1)} %get-tuple-element.4), kind=kOutput, calls=%fused_computation.4 | convolution fusion | flops 1613365248 | bytes 7347200 | tf_op jit(solution)/shard_map/dot_general | solution.py:45
  (26 shorter events, 0.4 us)
Async XLA Ops:
  7.2 21.1 %copy-start = (bf16[384,2048]{1,0:T(8,128)(2,1)S(1)}, bf16[384,2048]{1,0:T(8,128)(2,1)}, u32[]{:S(2)}) copy-start(bf16[384,2048]{1,0:T(8,128)(2,1)} %param.5) | copy-start | bytes 4718596
  7.2 183.5 %all-gather.2.cloned.1.call-start = ((), (), s32[]{:S(2)}) async-start(), calls=%async_computation.2 | async-start | bytes 8912896 | tf_op jit(solution)/shard_map/all_gather | solution.py:21
  11.5 28.5 %all-to-all-start = ((s32[32,1,24]{2,1,0:T(1,128)}), s32[32,1,24]{2,1,0:T(1,128)S(1)}, u32[]{:S(2)}, u32[]{:S(2)}) async-start(s32[32,1,24]{2,1,0:T(1,128)} %bitcast.10), calls=%async_computation | async-start | bytes 32768 | tf_op jit(solution)/shard_map/all_to_all | solution.py:67
  40.0 5.5 %copy-start.3 = (s32[1,8]{1,0:T(1,128)S(1)}, s32[1,8]{1,0:T(1,128)}, u32[]{:S(2)}) copy-start(s32[1,8]{1,0:T(1,128)} %param.7) | copy-start | bytes 100
  40.0 5.5 %copy-start.1 = (s32[1,16]{1,0:T(1,128)S(1)}, s32[1,16]{1,0:T(1,128)}, u32[]{:S(2)}) copy-start(s32[1,16]{1,0:T(1,128)} %param.8) | copy-start | bytes 196
  40.0 147.0 %copy-start.2 = (bf16[128,2048]{1,0:T(8,128)(2,1)S(1)}, bf16[128,2048]{1,0:T(8,128)(2,1)}, u32[]{:S(2)}) copy-start(bf16[128,2048]{1,0:T(8,128)(2,1)} %param.6) | copy-start | bytes 1572868
  40.0 147.0 %all-to-all-start.1 = ((bf16[32,24,2048]{2,1,0:T(8,128)(2,1)}), bf16[32,24,2048]{2,1,0:T(8,128)(2,1)}, u32[]{:S(2)}, u32[]{:S(2)}) async-start(bf16[32,24,2048]{2,1,0:T(8,128)(2,1)} %bitcast.69), calls=%async_computation.1 | async-start | bytes 6291456 | tf_op jit(solution)/shard_map/all_to_all | solution.py:66
Sparse Core Ops, SparseCore 0:
  11.0 91.3 all-gather.1
where the time goes:
time: 216 us; the launch traced here: 212 us
  waiting for transfers between devices  148 us (69%)
  starting transfers between devices  22.2 us (10%)
  between operations  14.2 us (7%)
  matrix products  11.9 us (6%)
  local copies, waits for them, and re-layouts  8.41 us (4%)
  other arithmetic  7.4 us (3%)
    all_to_all x1, waiting for transfers between devices, on_device(): lax.all_to_all(packed, 'region', split_axis=0, concat_axis=0, tiled=True)  139 us
    all_to_all x1, starting transfers between devices, on_device(): lax.all_to_all(slot_offsets, 'region', split_axis=0, concat_axis=0, tiled...  16.7 us
    all_to_all x1, waiting for transfers between devices, on_device(): lax.all_to_all(slot_offsets, 'region', split_axis=0, concat_axis=0, tiled...  8.16 us
    gather x1, local copies, waits for them, and re-layouts, on_device(): jnp.take(arrived, wanted_owner, axis=0).reshape(-1, feat_width)  6.17 us
    all_to_all x1, starting transfers between devices, on_device(): lax.all_to_all(packed, 'region', split_axis=0, concat_axis=0, tiled=True)  5.46 us
  transfers between devices with their start and end apart: 3, of which 2 were waited for; matrix products, arithmetic and copies ran while one was open for 6% of the time, Pallas kernels for 0%

commit v1 on v0

v1 whole, which is shorter than its diff:
```python
import functools

import jax
import jax.numpy as jnp
from jax import lax
from jax.experimental import pallas as pl
from jax.experimental.pallas import tpu as pltpu
from jax.sharding import PartitionSpec as P

MESH = pl.DeviceIdType.MESH
F32 = jnp.float32
BF16 = jnp.bfloat16

SHARPNESS = 0.05
SMOOTHING = 0.1
KEEP = 0.2


def kernel(
    chips, side,
    feat_hbm, mem_hbm, req_ref, own_ref, lab_ref,
    grad_hbm, new_hbm,
    feat, halves, ring, pair, labs, gath, old, part, hits, cand, score, logit, grad, mix, new,
    ring_send, ring_recv, lab_send, lab_recv, sib_send, sib_recv, ag_send, ag_recv, loc,
):
    crops, width = feat.shape
    half = width // 2
    rows = old.shape[1]
    long_arm = chips // 2
    region = lax.axis_index("region")
    group = lax.axis_index("group")
    chip = region // 2
    core = region % 2
    other = 1 - core
    sign = 1 - 2 * core
    gx, gy = group // side, group % side

    def chip_at(offset):
        return (chip + offset + chips) % chips

    def dev(chip_index, core_index, group_index):
        return (chip_index * 2 + core_index, group_index)

    my_cols = pl.ds(pl.multiple_of(core * half, half), half)
    other_cols = pl.ds(pl.multiple_of(other * half, half), half)

    local = [
        pltpu.make_async_copy(feat_hbm.at[:, my_cols], halves.at[0, pl.ds(0, crops)], loc.at[0]),
        pltpu.make_async_copy(feat_hbm.at[:, other_cols], halves.at[1, pl.ds(0, crops)], loc.at[1]),
        pltpu.make_async_copy(feat_hbm, feat, loc.at[2]),
        pltpu.make_async_copy(mem_hbm.at[:, my_cols], old.at[0], loc.at[3]),
        pltpu.make_async_copy(mem_hbm.at[:, other_cols], old.at[1], loc.at[4]),
        pltpu.make_async_copy(mem_hbm, gath.at[group], loc.at[5]),
    ]
    for copy in local:
        copy.start()
    pair[0] = lab_ref[...]

    def at_xy(dx, dy):
        return ((gx + dx + side) % side) * side + (gy + dy + side) % side

    partners = [dev(chip, other, group)]
    for step in (1, -1):
        partners.append(dev(chip_at(step), core, group))
        partners.append(dev(chip_at(step), other, group))
        partners.append((region, at_xy(step, 0)))
        partners.append((region, at_xy(0, step)))
    barrier = pltpu.get_barrier_semaphore()
    for partner in partners:
        pl.semaphore_signal(barrier, inc=1, device_id=partner, device_id_type=MESH)
    pl.semaphore_wait(barrier, len(partners))

    def remote(src, dst, send, recv, device):
        return pltpu.make_async_remote_copy(
            src_ref=src, dst_ref=dst, send_sem=send, recv_sem=recv, device_id=device, device_id_type=MESH
        )

    sibling = dev(chip, other, group)
    swap = [
        remote(pair.at[0], pair.at[1], sib_send.at[0], sib_recv.at[0], sibling),
        remote(feat_hbm.at[:, other_cols], halves.at[0, pl.ds(crops, crops)], sib_send.at[1], sib_recv.at[1], sibling),
        remote(feat_hbm.at[:, my_cols], halves.at[1, pl.ds(crops, crops)], sib_send.at[2], sib_recv.at[2], sibling),
    ]
    for copy in swap:
        copy.start()

    offs = (0, -1, 1, 2)

    def block(h, i, j):
        def off(k):
            return k
        dx, dy = (i, j) if h == 0 else (j, i)
        return at_xy(dx, dy)

    def ag_copy(h, index, src_block, rows_of, device_block, own=False):
        cols = pl.ds(h * half, half)
        dst = gath.at[src_block, rows_of, cols]
        src = mem_hbm.at[rows_of, cols] if own else dst
        return remote(src, dst, ag_send.at[h, index], ag_recv.at[h, index], (region, device_block))

    full = pl.ds(0, rows)
    part_of = {1: pl.ds(0, rows // 2), -1: pl.ds(rows // 2, rows // 2)}
    way = {1: 0, -1: 1}

    def p1(h, u, recv=False):
        return ag_copy(h, way[u], block(h, -u, 0) if recv else block(h, 0, 0), full, block(h, u, 0), own=not recv)

    def p2(h, u, recv=False):
        return ag_copy(h, 2 + way[u], block(h, -2 * u if recv else -u, 0), part_of[u], block(h, u, 0))

    def q1(h, a, u, recv=False):
        return ag_copy(
            h, 4 + 2 * a + way[u], block(h, offs[a], -u if recv else 0), full, block(h, 0, u), own=(a == 0 and not recv)
        )

    def q2(h, a, u, recv=False):
        return ag_copy(
            h, 12 + 2 * a + way[u], block(h, offs[a], -2 * u if recv else -u), part_of[u], block(h, 0, u)
        )

    both = (1, -1)

    def gather_round0():
        for u in both:
            for h in range(2):
                p1(h, u).start()
        for u in both:
            for h in range(2):
                q1(h, 0, u).start()

    def gather_round1():
        for h in range(2):
            for u, a in ((1, 1), (-1, 2)):
                p1(h, u, True).wait_recv()
                p2(h, u).start()
                for v in both:
                    q1(h, a, v).start()
        for h in range(2):
            for u in both:
                q1(h, 0, u, True).wait_recv()
                q2(h, 0, u).start()

    def gather_round2():
        for h in range(2):
            for u in both:
                p2(h, u, True).wait_recv()
            for u in both:
                q1(h, 3, u).start()
        for h in range(2):
            for a in (1, 2):
                for u in both:
                    q1(h, a, u, True).wait_recv()
                    q2(h, a, u).start()

    def gather_round3():
        for h in range(2):
            for u in both:
                q1(h, 3, u, True).wait_recv()
                q2(h, 3, u).start()

    def gather_round4():
        for h in range(2):
            for a in range(4):
                for u in both:
                    q2(h, a, u, True).wait_recv()
        local[5].wait()

    def gather_sent():
        for h in range(2):
            for u in both:
                p1(h, u).wait_send()
                p2(h, u).wait_send()
                for a in range(4):
                    q1(h, a, u).wait_send()
                    q2(h, a, u).wait_send()

    gather_round0()

    places = lax.broadcasted_iota(jnp.int32, (rows, crops), 0)

    def hit(label_row, target):
        return jnp.where(places == label_row - target * rows, 1.0, 0.0)

    def own_sums(target, which):
        pick = jnp.concatenate([hit(pair[0], target), hit(pair[1], target)], axis=1).astype(BF16)
        return jnp.dot(pick, halves[which], preferred_element_type=F32)

    def count(label_pair):
        hits[...] += hit(label_pair[0], region) + hit(label_pair[1], region)

    def ring_copy(t, arm, e, device):
        return remote(
            ring.at[arm, e, t], ring.at[arm, e, t + 1], ring_send.at[arm, e, t], ring_recv.at[arm, e, t + 1], device
        )

    def ring_target(t, arm, e):
        towards = sign * (1 - 2 * arm)
        distance = long_arm - arm - t
        goal = chip_at(towards * distance) * 2 + core + e * sign
        last = (t + arm) // (long_arm - 1)
        nearest = dev(chip_at(towards), core + last * e * sign, group)
        return goal, nearest

    def lab_copy(t, arm):
        towards = sign * (1 - 2 * arm)
        return remote(
            labs.at[arm, t], labs.at[arm, t + 1], lab_send.at[arm, t], lab_recv.at[arm, t + 1],
            dev(chip_at(towards), core, group),
        )

    swap[0].wait_recv()
    for arm in range(2):
        labs[arm, 0] = pair[...]
        lab_copy(0, arm).start()
    local[0].wait()
    swap[1].wait_recv()

    @pl.loop(0, 4)
    def _(q):
        arm, e = q % 2, q // 2
        goal, nearest = ring_target(0, arm, e)
        ring[arm, e, 0] = own_sums(goal, 0).astype(BF16)
        ring_copy(0, arm, e, nearest).start()

    hits[...] = jnp.zeros_like(hits)
    count(pair)

    def take_candidates():
        for k in range(8):
            cand[k * rows:(k + 1) * rows, :] = gath[own_ref[0, req_ref[0, k]]]

    def scores():
        local[2].wait()

        @pl.loop(0, 4)
        def _(n):
            span = pl.ds(pl.multiple_of(n * 256, 256), 256)
            score[:, span] = lax.dot_general(
                feat[...], cand[span, :], (((1,), (1,)), ((), ())), preferred_element_type=F32
            ) * (1.0 / SHARPNESS)

    def softmax():
        total = cand.shape[0]

        @pl.loop(0, crops // 64)
        def _(n):
            span = pl.ds(pl.multiple_of(n * 64, 64), 64)
            s = score[span, :]
            expo = jnp.exp(s - jnp.max(s, axis=1, keepdims=True))
            prob = expo / jnp.sum(expo, axis=1, keepdims=True)
            column = lax.broadcasted_iota(jnp.int32, s.shape, 1)
            target = jnp.where(column < rows, (1.0 - SMOOTHING) / rows, 0.0) + SMOOTHING / total
            logit[span, :] = ((prob - target) * (1.0 / SHARPNESS)).astype(BF16)

    def grads():
        @pl.loop(0, width // 256)
        def _(n):
            span = pl.ds(pl.multiple_of(n * 256, 256), 256)
            grad[:, span] = jnp.dot(logit[...], cand[:, span], preferred_element_type=F32).astype(BF16)

    grad_out = pltpu.make_async_copy(grad, grad_hbm, loc.at[6])

    @pl.loop(1, long_arm)
    def _(t):
        @pl.loop(0, 4)
        def _(q):
            arm, e = q % 2, q // 2

            @pl.when(t + arm < long_arm)
            def _():
                goal, nearest = ring_target(t, arm, e)
                part[...] = own_sums(goal, 0)
                ring_copy(t - 1, arm, e, nearest).wait_recv()
                ring[arm, e, t] = (part[...] + ring[arm, e, t].astype(F32)).astype(BF16)
                ring_copy(t, arm, e, nearest).start()

        for arm in range(2):
            @pl.when(t + arm < long_arm)
            def _():
                lab_copy(t - 1, arm).wait_recv()
                lab_copy(t, arm).start()
                count(labs.at[arm, t])

        @pl.when(t == 1)
        def _():
            gather_round1()

        @pl.when(t == 2)
        def _():
            gather_round2()

        @pl.when(t == 3)
        def _():
            gather_round3()

        @pl.when(t == 4)
        def _():
            gather_round4()
            take_candidates()

        @pl.when(t == 5)
        def _():
            scores()
            softmax()

        @pl.when(t == 6)
        def _():
            grads()
            grad_out.start()

    lab_copy(long_arm - 1, 0).wait_recv()
    count(labs.at[0, long_arm])
    lab_copy(long_arm - 2, 1).wait_recv()
    count(labs.at[1, long_arm - 1])
    counts = jnp.sum(hits[...], axis=1, keepdims=True)
    inverse = 1.0 / jnp.maximum(counts, 1.0)
    local[1].wait()
    swap[2].wait_recv()
    local[3].wait()
    local[4].wait()
    square = jnp.zeros((rows, 1), F32)
    for which in range(2):
        part[...] = own_sums(region, which)
        for arm in range(2):
            ring_copy(long_arm - 1 - arm, arm, which, sibling).wait_recv()
        sums = part[...] + ring[0, which, long_arm].astype(F32) + ring[1, which, long_arm - 1].astype(F32)
        before = old[which].astype(F32)
        mixed = jnp.where(counts > 0, KEEP * before + (1.0 - KEEP) * (sums * inverse), before)
        mix[which] = mixed
        square += jnp.sum(mixed * mixed, axis=1, keepdims=True)
    scale = lax.rsqrt(square * (1.0 / width) + 1e-06) * width ** (-0.5)
    outs = []
    for which, cols in ((0, my_cols), (1, other_cols)):
        new[which] = (mix[which] * scale).astype(BF16)
        copy = pltpu.make_async_copy(new.at[which], new_hbm.at[:, cols], loc.at[7 + which])
        copy.start()
        outs.append(copy)

    for copy in swap:
        copy.wait_send()
    gather_sent()
    for arm in range(2):
        @pl.loop(0, long_arm - arm)
        def _(t):
            lab_copy(t, arm).wait_send()
            for e in range(2):
                ring_copy(t, arm, e, sibling).wait_send()
    grad_out.wait()
    for copy in outs:
        copy.wait()


def solution(mesh):
    regions, groups = mesh.shape["region"], mesh.shape["group"]
    chips = regions // 2
    side = int(round(groups ** 0.5))

    def on_device(features, memory, requests, owners, labels):
        crops, width = features.shape
        rows = memory.shape[0]
        half = width // 2
        arm = chips // 2
        total = requests.shape[1] * rows
        any_spec = pl.BlockSpec(memory_space=pl.ANY)
        smem = pl.BlockSpec(memory_space=pltpu.SMEM)
        vmem = pl.BlockSpec(memory_space=pltpu.VMEM)
        dma = pltpu.SemaphoreType.DMA
        return pl.pallas_call(
            functools.partial(kernel, chips, side),
            out_shape=(
                jax.ShapeDtypeStruct((crops, width), BF16),
                jax.ShapeDtypeStruct((rows, width), BF16),
            ),
            in_specs=[any_spec, any_spec, smem, smem, vmem],
            out_specs=(any_spec, any_spec),
            scratch_shapes=[
                pltpu.VMEM((crops, width), BF16),
                pltpu.VMEM((2, 2 * crops, half), BF16),
                pltpu.VMEM((2, 2, arm + 1, rows, half), BF16),
                pltpu.VMEM((2, 1, crops), jnp.int32),
                pltpu.VMEM((2, arm + 1, 2, 1, crops), jnp.int32),
                pltpu.VMEM((groups, rows, width), BF16),
                pltpu.VMEM((2, rows, half), BF16),
                pltpu.VMEM((rows, half), F32),
                pltpu.VMEM((rows, crops), F32),
                pltpu.VMEM((total, width), BF16),
                pltpu.VMEM((crops, total), F32),
                pltpu.VMEM((crops, total), BF16),
                pltpu.VMEM((crops, width), BF16),
                pltpu.VMEM((2, rows, half), F32),
                pltpu.VMEM((2, rows, half), BF16),
                dma((2, 2, arm + 1)),
                dma((2, 2, arm + 1)),
                dma((2, arm + 1)),
                dma((2, arm + 1)),
                dma((3,)),
                dma((3,)),
                dma((2, 20)),
                dma((2, 20)),
                dma((9,)),
            ],
            compiler_params=pltpu.CompilerParams(
                collective_id=0, has_side_effects=True, vmem_limit_bytes=56 << 20
            ),
        )(features, memory, requests, owners, labels)

    both = P(("region", "group"), None)
    return jax.shard_map(
        on_device,
        mesh=mesh,
        in_specs=(both, both, both, P("region", None), both),
        out_specs=(both, both),
        check_vma=False,
    )
```

time: 216 us -> 111 us (0.51); the launches traced: 212 us -> 110 us
  waiting for transfers between devices: 148 us -> 0 us
  Pallas kernels: 0 us -> 106 us
  starting transfers between devices: 22.2 us -> 0 us
  between operations: 14.2 us -> 0.65 us
  matrix products: 11.9 us -> 0 us
  other arithmetic: 7.4 us -> 0 us
  local copies, waits for them, and re-layouts: 8.41 us -> 3.58 us
    all_to_all x2 -> x0, waiting for transfers between devices: 147 us -> none  [the longest x1 139 us: on_device(): lax.all_to_all(packed, 'region', split_axis=0, concat_axis=0, tiled=True)]
    pallas_call x0 -> x1, Pallas kernels: none -> 106 us  [on_device(): pl.pallas_call(functools.partial(kernel, chips, side), out_shape=(jax.Sha...]
    all_to_all x2 -> x0, starting transfers between devices: 22.2 us -> none  [the longest x1 16.7 us: on_device(): lax.all_to_all(slot_offsets, 'region', split_axis=0, concat_axis=0, tiled...]
    dot_general x4 -> x0, matrix products: 11.9 us -> none  [the longest x1 3.54 us: on_device(): jnp.dot(slot_match.astype(jnp.bfloat16), features, preferred_element_type...]
    gather x2 -> x0, local copies, waits for them, and re-layouts: 6.81 us -> none  [the longest x1 6.17 us: on_device(): jnp.take(arrived, wanted_owner, axis=0).reshape(-1, feat_width)]
    unnamed x8 -> x4, local copies, waits for them, and re-layouts: 0.02 us -> 3.58 us
    select_n x5 -> x0, other arithmetic: 2.66 us -> none  [the longest x2 2.64 us: on_device(): jnp.take(arrived, wanted_owner, axis=0).reshape(-1, feat_width)]
  transfers between devices with their start and end apart: 3 -> 0, of which waited for: 2 -> 0; matrix products, arithmetic and copies ran while one was open for 6% -> 0% of each run, Pallas kernels for 0% -> 0%
where the time goes in v1:
time: 111 us; the launch traced here: 110 us
  Pallas kernels  106 us (95%)
  local copies, waits for them, and re-layouts  3.58 us (3%)
    pallas_call x1, Pallas kernels, on_device(): pl.pallas_call(functools.partial(kernel, chips, side), out_shape=(jax.Sha...  106 us
    unnamed x4, local copies, waits for them, and re-layouts  3.58 us

profile of v1, /device:TPU:1, one launch (start us, length us, event | category | flops | bytes accessed | tf_op | source)
XLA Modules:
  0.0 110.1 jit_solution(11655129409411380743)
XLA Ops:
  0.6 105.9 %shard_map.68 = (bf16[384,2048]{1,0:T(8,128)(2,1)}, bf16[128,2048]{1,0:T(8,128)(2,1)}) custom-call(bf16[384,2048]{1,0:T(8,128)(2,1)} %feat_hbm.1, bf16[128,2048]{1,0:T(8,128)(2,1)} %mem_hbm.1, s32[1,8]{1,0:T(1,128)} %req_ref.1, s32[1,16]{1,0:T(1,128)} %own_ref.1, s32[1,384]{1,0:T(1,128)} %lab_ref.1), custom_call_target="tpu_custom_call" | custom-call | tf_op jit(solution)/shard_map/pallas_call | solution.py:368
  106.5 0.0 copy-start
  106.5 2.8 %copy.9 = bf16[384,2048]{1,0:T(8,128)(2,1)} copy(bf16[384,2048]{1,0:T(8,128)(2,1)} %get-tuple-element.4) | data formatting | bytes 3145728
  109.3 0.0 copy-done
  109.3 0.8 copy.10
Async XLA Ops:
  106.5 2.8 %copy-start = (bf16[128,2048]{1,0:T(8,128)(2,1)S(1)}, bf16[128,2048]{1,0:T(8,128)(2,1)}, u32[]{:S(2)}) copy-start(bf16[128,2048]{1,0:T(8,128)(2,1)} %get-tuple-element.5) | copy-start | bytes 1572868

commit v2 on v1

--- a/solution.py
+++ b/solution.py
@@ -20,12 +20,14 @@
     chips, side,
     feat_hbm, mem_hbm, req_ref, own_ref, lab_ref,
     grad_hbm, new_hbm,
-    feat, halves, ring, pair, labs, gath, old, part, hits, cand, score, logit, grad, mix, new,
-    ring_send, ring_recv, lab_send, lab_recv, sib_send, sib_recv, ag_send, ag_recv, loc,
+    feat, halves, ring, packs, near, far, pair, labs, gath, old, part, hits, cand, score, logit, grad, mix, new,
+    ring_send, ring_recv, pack_send, pack_recv, lab_send, lab_recv, sib_send, sib_recv, ag_send, ag_recv, loc,
 ):
     crops, width = feat.shape
     half = width // 2
     rows = old.shape[1]
+    packed = near.shape[1] // 2
+    slots = packed // 2
     long_arm = chips // 2
     region = lax.axis_index("region")
     group = lax.axis_index("group")
@@ -54,7 +56,20 @@
     ]
     for copy in local:
         copy.start()
-    pair[0] = lab_ref[...]
+
+    label = lab_ref[...]
+    label_region = lax.shift_right_logical(label, jnp.int32(rows.bit_length() - 1))
+    of_region = jnp.where(
+        lax.broadcasted_iota(jnp.int32, (2 * chips, crops), 0) == label_region, 1.0, 0.0
+    )
+    before_crop = jnp.where(
+        lax.broadcasted_iota(jnp.int32, (crops, crops), 0) < lax.broadcasted_iota(jnp.int32, (crops, crops), 1),
+        1.0, 0.0,
+    ).astype(BF16)
+    earlier = jnp.dot(of_region.astype(BF16), before_crop, preferred_element_type=F32)
+    rank = jnp.sum(earlier * of_region, axis=0, keepdims=True).astype(jnp.int32)
+    pair[0, :, 0:crops] = label
+    pair[0, :, crops:2 * crops] = label_region * slots + rank
 
     def at_xy(dx, dy):
         return ((gx + dx + side) % side) * side + (gy + dy + side) % side
@@ -81,8 +96,44 @@
         remote(feat_hbm.at[:, other_cols], halves.at[0, pl.ds(crops, crops)], sib_send.at[1], sib_recv.at[1], sibling),
         remote(feat_hbm.at[:, my_cols], halves.at[1, pl.ds(crops, crops)], sib_send.at[2], sib_recv.at[2], sibling),
     ]
-    for copy in swap:
-        copy.start()
+    swap[0].start()
+
+    def pack_copy(stage, arm, e):
+        towards = sign * (1 - 2 * arm) * (1 - 2 * e)
+        place = pl.ds(pl.multiple_of(e * packed, packed), packed)
+        landing = near if stage == 0 else far
+        return remote(
+            packs.at[stage, arm, e], landing.at[arm, place],
+            pack_send.at[arm, 2 * stage + e], pack_recv.at[arm, 2 * stage + e],
+            dev(chip_at(towards), core + e * sign, group),
+        )
+
+    def forward_copy(arm):
+        towards = sign * (1 - 2 * arm)
+        return remote(
+            near.at[arm], far.at[arm, pl.ds(2 * packed, 2 * packed)], pack_send.at[arm, 4], pack_recv.at[arm, 4],
+            dev(chip_at(towards), core, group),
+        )
+
+    def send_packed(stage):
+        @pl.loop(0, 4)
+        def _(q):
+            arm, e = q % 2, q // 2
+            towards = sign * (1 - 2 * arm) * (1 - 2 * e)
+            goal = chip_at(towards * (long_arm - arm - stage))
+            take = jnp.where(
+                lax.broadcasted_iota(jnp.int32, (packed, crops), 0) + goal * packed == pair[0, :, crops:2 * crops],
+                1.0, 0.0,
+            ).astype(BF16)
+            packs[stage, arm, e] = jnp.dot(
+                take, halves[e, 0:crops, :], preferred_element_type=F32
+            ).astype(BF16)
+            pack_copy(stage, arm, e).start()
+
+    local[0].wait()
+    local[1].wait()
+    send_packed(0)
+    swap[1].start()
 
     offs = (0, -1, 1, 2)
 
@@ -175,6 +226,8 @@
                     q2(h, a, u).wait_send()
 
     gather_round0()
+    send_packed(1)
+    swap[2].start()
 
     places = lax.broadcasted_iota(jnp.int32, (rows, crops), 0)
 
@@ -182,15 +235,32 @@
         return jnp.where(places == label_row - target * rows, 1.0, 0.0)
 
     def own_sums(target, which):
-        pick = jnp.concatenate([hit(pair[0], target), hit(pair[1], target)], axis=1).astype(BF16)
+        pick = jnp.concatenate([hit(pair[k, :, 0:crops], target) for k in range(2)], axis=1).astype(BF16)
         return jnp.dot(pick, halves[which], preferred_element_type=F32)
 
     def count(label_pair):
-        hits[...] += hit(label_pair[0], region) + hit(label_pair[1], region)
+        hits[...] += hit(label_pair[0, :, 0:crops], region) + hit(label_pair[1, :, 0:crops], region)
+
+    def spread(arm, target):
+        sources = [(labs.at[arm, hop], k) for hop in (1, 2) for k in range(2)]
+        first = target // 2 * packed
+        put, take = [], []
+        for n, (source, k) in enumerate(sources):
+            slot = source[k, :, crops:2 * crops] - first
+            slot = jnp.where((slot >= 0) & (slot < packed), slot + n * packed, -1)
+            place = lax.broadcasted_iota(jnp.int32, (4 * packed, crops), 0)
+            take.append(jnp.where(place == slot, 1.0, 0.0).astype(BF16))
+            put.append(hit(source[k, :, 0:crops], target).astype(BF16))
+        move = lax.dot_general(
+            jnp.concatenate(put, axis=1), jnp.concatenate(take, axis=1), (((1,), (1,)), ((), ())),
+            preferred_element_type=F32,
+        ).astype(BF16)
+        return jnp.dot(move, far[arm], preferred_element_type=F32)
 
     def ring_copy(t, arm, e, device):
         return remote(
-            ring.at[arm, e, t], ring.at[arm, e, t + 1], ring_send.at[arm, e, t], ring_recv.at[arm, e, t + 1], device
+            ring.at[arm, e, t - 2], ring.at[arm, e, t - 1], ring_send.at[arm, e, t - 2], ring_recv.at[arm, e, t - 1],
+            device,
         )
 
     def ring_target(t, arm, e):
@@ -212,16 +282,6 @@
     for arm in range(2):
         labs[arm, 0] = pair[...]
         lab_copy(0, arm).start()
-    local[0].wait()
-    swap[1].wait_recv()
-
-    @pl.loop(0, 4)
-    def _(q):
-        arm, e = q % 2, q // 2
-        goal, nearest = ring_target(0, arm, e)
-        ring[arm, e, 0] = own_sums(goal, 0).astype(BF16)
-        ring_copy(0, arm, e, nearest).start()
-
     hits[...] = jnp.zeros_like(hits)
     count(pair)
 
@@ -260,7 +320,36 @@
 
     grad_out = pltpu.make_async_copy(grad, grad_hbm, loc.at[6])
 
-    @pl.loop(1, long_arm)
+    def pass_labels(t, arm):
+        lab_copy(t - 1, arm).wait_recv()
+        lab_copy(t, arm).start()
+        count(labs.at[arm, t])
+
+    for arm in range(2):
+        for e in range(2):
+            pack_copy(0, arm, e).wait_recv()
+        forward_copy(arm).start()
+        pass_labels(1, arm)
+    gather_round1()
+    swap[1].wait_recv()
+
+    for arm in range(2):
+        for e in range(2):
+            pack_copy(1, arm, e).wait_recv()
+        forward_copy(arm).wait_recv()
+        pass_labels(2, arm)
+
+    @pl.loop(0, 4)
+    def _(q):
+        arm, e = q % 2, q // 2
+        goal, nearest = ring_target(2, arm, e)
+        part[...] = own_sums(goal, 0)
+        ring[arm, e, 0] = (part[...] + spread(arm, goal)).astype(BF16)
+        ring_copy(2, arm, e, nearest).start()
+
+    gather_round2()
+
+    @pl.loop(3, long_arm)
     def _(t):
         @pl.loop(0, 4)
         def _(q):
@@ -271,23 +360,13 @@
                 goal, nearest = ring_target(t, arm, e)
                 part[...] = own_sums(goal, 0)
                 ring_copy(t - 1, arm, e, nearest).wait_recv()
-                ring[arm, e, t] = (part[...] + ring[arm, e, t].astype(F32)).astype(BF16)
+                ring[arm, e, t - 2] = (part[...] + ring[arm, e, t - 2].astype(F32)).astype(BF16)
                 ring_copy(t, arm, e, nearest).start()
 
         for arm in range(2):
             @pl.when(t + arm < long_arm)
             def _():
-                lab_copy(t - 1, arm).wait_recv()
-                lab_copy(t, arm).start()
-                count(labs.at[arm, t])
-
-        @pl.when(t == 1)
-        def _():
-            gather_round1()
-
-        @pl.when(t == 2)
-        def _():
-            gather_round2()
+                pass_labels(t, arm)
 
         @pl.when(t == 3)
         def _():
@@ -314,7 +393,6 @@
     count(labs.at[1, long_arm - 1])
     counts = jnp.sum(hits[...], axis=1, keepdims=True)
     inverse = 1.0 / jnp.maximum(counts, 1.0)
-    local[1].wait()
     swap[2].wait_recv()
     local[3].wait()
     local[4].wait()
@@ -323,7 +401,7 @@
         part[...] = own_sums(region, which)
         for arm in range(2):
             ring_copy(long_arm - 1 - arm, arm, which, sibling).wait_recv()
-        sums = part[...] + ring[0, which, long_arm].astype(F32) + ring[1, which, long_arm - 1].astype(F32)
+        sums = part[...] + ring[0, which, long_arm - 2].astype(F32) + ring[1, which, long_arm - 3].astype(F32)
         before = old[which].astype(F32)
         mixed = jnp.where(counts > 0, KEEP * before + (1.0 - KEEP) * (sums * inverse), before)
         mix[which] = mixed
@@ -340,13 +418,35 @@
         copy.wait_send()
     gather_sent()
     for arm in range(2):
+        forward_copy(arm).wait_send()
+        for e in range(2):
+            for stage in range(2):
+                pack_copy(stage, arm, e).wait_send()
+
         @pl.loop(0, long_arm - arm)
         def _(t):
             lab_copy(t, arm).wait_send()
+
+        @pl.loop(2, long_arm - arm)
+        def _(t):
             for e in range(2):
                 ring_copy(t, arm, e, sibling).wait_send()
     grad_out.wait()
     for copy in outs:
+        copy.wait()
+
+
+def hand_over(grad_in, new_in, grad_out, new_out, sem):
+    crops, rows = grad_in.shape[0], new_in.shape[0]
+    piece = rows // 2
+    copies = []
+    for source, target, count in ((grad_in, grad_out, crops), (new_in, new_out, rows)):
+        for first in range(0, count, piece):
+            span = pl.ds(first, piece)
+            copies.append(pltpu.make_async_copy(source.at[span], target.at[span], sem.at[len(copies)]))
+    for copy in copies:
+        copy.start()
+    for copy in copies:
         copy.wait()
 
 
@@ -365,20 +465,25 @@
         smem = pl.BlockSpec(memory_space=pltpu.SMEM)
         vmem = pl.BlockSpec(memory_space=pltpu.VMEM)
         dma = pltpu.SemaphoreType.DMA
-        return pl.pallas_call(
+        shapes = (
+            jax.ShapeDtypeStruct((crops, width), BF16),
+            jax.ShapeDtypeStruct((rows, width), BF16),
+        )
+        packed = 2 * max(2, 2 * crops // regions)
+        results = pl.pallas_call(
             functools.partial(kernel, chips, side),
-            out_shape=(
-                jax.ShapeDtypeStruct((crops, width), BF16),
-                jax.ShapeDtypeStruct((rows, width), BF16),
-            ),
+            out_shape=shapes,
             in_specs=[any_spec, any_spec, smem, smem, vmem],
             out_specs=(any_spec, any_spec),
             scratch_shapes=[
                 pltpu.VMEM((crops, width), BF16),
                 pltpu.VMEM((2, 2 * crops, half), BF16),
-                pltpu.VMEM((2, 2, arm + 1, rows, half), BF16),
-                pltpu.VMEM((2, 1, crops), jnp.int32),
-                pltpu.VMEM((2, arm + 1, 2, 1, crops), jnp.int32),
+                pltpu.VMEM((2, 2, arm - 1, rows, half), BF16),
+                pltpu.VMEM((2, 2, 2, packed, half), BF16),
+                pltpu.VMEM((2, 2 * packed, half), BF16),
+                pltpu.VMEM((2, 4 * packed, half), BF16),
+                pltpu.VMEM((2, 1, 2 * crops), jnp.int32),
+                pltpu.VMEM((2, arm + 1, 2, 1, 2 * crops), jnp.int32),
                 pltpu.VMEM((groups, rows, width), BF16),
                 pltpu.VMEM((2, rows, half), BF16),
                 pltpu.VMEM((rows, half), F32),
@@ -389,8 +494,10 @@
                 pltpu.VMEM((crops, width), BF16),
                 pltpu.VMEM((2, rows, half), F32),
                 pltpu.VMEM((2, rows, half), BF16),
-                dma((2, 2, arm + 1)),
-                dma((2, 2, arm + 1)),
+                dma((2, 2, arm - 1)),
+                dma((2, 2, arm - 1)),
+                dma((2, 5)),
+                dma((2, 5)),
                 dma((2, arm + 1)),
                 dma((2, arm + 1)),
                 dma((3,)),
@@ -403,6 +510,14 @@
                 collective_id=0, has_side_effects=True, vmem_limit_bytes=56 << 20
             ),
         )(features, memory, requests, owners, labels)
+        pieces = 2 * (crops + rows) // rows
+        return pl.pallas_call(
+            hand_over,
+            out_shape=shapes,
+            in_specs=[any_spec, any_spec],
+            out_specs=(any_spec, any_spec),
+            scratch_shapes=[dma((pieces,))],
+        )(*results)
 
     both = P(("region", "group"), None)
     return jax.shard_map(

time: 111 us -> 165 us (1.49)
  Pallas kernels: 106 us -> 164 us
  local copies, waits for them, and re-layouts: 3.58 us -> 0 us
    pallas_call x1 -> x2, Pallas kernels: 106 us -> 164 us  [the longest x1 99.4 us: on_device(): pl.pallas_call(functools.partial(kernel, chips, side), out_shape=shapes,...]
    unnamed x4 -> x0, local copies, waits for them, and re-layouts: 3.58 us -> none
where the time goes in v2:
time: 165 us
  Pallas kernels  164 us (99%)
    pallas_call x1, Pallas kernels, on_device(): pl.pallas_call(functools.partial(kernel, chips, side), out_shape=shapes,...  99.4 us
    pallas_call x1, Pallas kernels, on_device(): pl.pallas_call(hand_over, out_shape=shapes, in_specs=[any_spec, any_spec]...  64.7 us

profile of v2, /device:TPU:1, one launch (start us, length us, event | category | flops | bytes accessed | tf_op | source)
XLA Modules:
  0.0 164.7 jit_solution(17648135217433390374)
XLA Ops:
  0.6 99.4 %shard_map.68 = (bf16[384,2048]{1,0:T(8,128)(2,1)}, bf16[128,2048]{1,0:T(8,128)(2,1)}) custom-call(bf16[384,2048]{1,0:T(8,128)(2,1)} %feat_hbm.1, bf16[128,2048]{1,0:T(8,128)(2,1)} %mem_hbm.1, s32[1,8]{1,0:T(1,128)} %req_ref.1, s32[1,16]{1,0:T(1,128)} %own_ref.1, s32[1,384]{1,0:T(1,128)} %lab_ref.1), custom_call_target="tpu_custom_call" | custom-call | tf_op jit(solution)/shard_map/pallas_call | solution.py:473
  100.0 64.7 %shard_map.69 = (bf16[384,2048]{1,0:T(8,128)(2,1)}, bf16[128,2048]{1,0:T(8,128)(2,1)}) custom-call(bf16[384,2048]{1,0:T(8,128)(2,1)} %get-tuple-element.4.grad_in, bf16[128,2048]{1,0:T(8,128)(2,1)} %get-tuple-element.5.new_in), custom_call_target="tpu_custom_call" | custom-call | tf_op jit(solution)/shard_map/pallas_call | solution.py:514

commit v3 on v2

--- a/solution.py
+++ b/solution.py
@@ -19,8 +19,8 @@
 def kernel(
     chips, side,
     feat_hbm, mem_hbm, req_ref, own_ref, lab_ref,
-    grad_hbm, new_hbm,
-    feat, halves, ring, packs, near, far, pair, labs, gath, old, part, hits, cand, score, logit, grad, mix, new,
+    grad, new,
+    feat, halves, ring, packs, near, far, pair, labs, gath, old, part, move, hits, cand, score, logit, mix,
     ring_send, ring_recv, pack_send, pack_recv, lab_send, lab_recv, sib_send, sib_recv, ag_send, ag_recv, loc,
 ):
     crops, width = feat.shape
@@ -46,6 +46,19 @@
     my_cols = pl.ds(pl.multiple_of(core * half, half), half)
     other_cols = pl.ds(pl.multiple_of(other * half, half), half)
 
+    def at_xy(dx, dy):
+        return ((gx + dx + side) % side) * side + (gy + dy + side) % side
+
+    partners = [dev(chip, other, group)]
+    for step in (1, -1):
+        partners.append(dev(chip_at(step), core, group))
+        partners.append(dev(chip_at(step), other, group))
+        partners.append((region, at_xy(step, 0)))
+        partners.append((region, at_xy(0, step)))
+    barrier = pltpu.get_barrier_semaphore()
+    for partner in partners:
+        pl.semaphore_signal(barrier, inc=1, device_id=partner, device_id_type=MESH)
+
     local = [
         pltpu.make_async_copy(feat_hbm.at[:, my_cols], halves.at[0, pl.ds(0, crops)], loc.at[0]),
         pltpu.make_async_copy(feat_hbm.at[:, other_cols], halves.at[1, pl.ds(0, crops)], loc.at[1]),
@@ -71,18 +84,6 @@
     pair[0, :, 0:crops] = label
     pair[0, :, crops:2 * crops] = label_region * slots + rank
 
-    def at_xy(dx, dy):
-        return ((gx + dx + side) % side) * side + (gy + dy + side) % side
-
-    partners = [dev(chip, other, group)]
-    for step in (1, -1):
-        partners.append(dev(chip_at(step), core, group))
-        partners.append(dev(chip_at(step), other, group))
-        partners.append((region, at_xy(step, 0)))
-        partners.append((region, at_xy(0, step)))
-    barrier = pltpu.get_barrier_semaphore()
-    for partner in partners:
-        pl.semaphore_signal(barrier, inc=1, device_id=partner, device_id_type=MESH)
     pl.semaphore_wait(barrier, len(partners))
 
     def remote(src, dst, send, recv, device):
@@ -115,10 +116,9 @@
             dev(chip_at(towards), core, group),
         )
 
-    def send_packed(stage):
-        @pl.loop(0, 4)
-        def _(q):
-            arm, e = q % 2, q // 2
+    def send_packed(stage, arm):
+        @pl.loop(0, 2)
+        def _(e):
             towards = sign * (1 - 2 * arm) * (1 - 2 * e)
             goal = chip_at(towards * (long_arm - arm - stage))
             take = jnp.where(
@@ -132,8 +132,7 @@
 
     local[0].wait()
     local[1].wait()
-    send_packed(0)
-    swap[1].start()
+    send_packed(0, 0)
 
     offs = (0, -1, 1, 2)
 
@@ -186,6 +185,8 @@
                 p2(h, u).start()
                 for v in both:
                     q1(h, a, v).start()
+
+    def gather_round1b():
         for h in range(2):
             for u in both:
                 q1(h, 0, u, True).wait_recv()
@@ -226,8 +227,10 @@
                     q2(h, a, u).wait_send()
 
     gather_round0()
-    send_packed(1)
+    send_packed(1, 0)
+    swap[1].start()
     swap[2].start()
+    send_packed(0, 1)
 
     places = lax.broadcasted_iota(jnp.int32, (rows, crops), 0)
 
@@ -241,7 +244,7 @@
     def count(label_pair):
         hits[...] += hit(label_pair[0, :, 0:crops], region) + hit(label_pair[1, :, 0:crops], region)
 
-    def spread(arm, target):
+    def moves(arm, target):
         sources = [(labs.at[arm, hop], k) for hop in (1, 2) for k in range(2)]
         first = target // 2 * packed
         put, take = [], []
@@ -251,11 +254,10 @@
             place = lax.broadcasted_iota(jnp.int32, (4 * packed, crops), 0)
             take.append(jnp.where(place == slot, 1.0, 0.0).astype(BF16))
             put.append(hit(source[k, :, 0:crops], target).astype(BF16))
-        move = lax.dot_general(
+        return lax.dot_general(
             jnp.concatenate(put, axis=1), jnp.concatenate(take, axis=1), (((1,), (1,)), ((), ())),
             preferred_element_type=F32,
         ).astype(BF16)
-        return jnp.dot(move, far[arm], preferred_element_type=F32)
 
     def ring_copy(t, arm, e, device):
         return remote(
@@ -318,8 +320,6 @@
             span = pl.ds(pl.multiple_of(n * 256, 256), 256)
             grad[:, span] = jnp.dot(logit[...], cand[:, span], preferred_element_type=F32).astype(BF16)
 
-    grad_out = pltpu.make_async_copy(grad, grad_hbm, loc.at[6])
-
     def pass_labels(t, arm):
         lab_copy(t - 1, arm).wait_recv()
         lab_copy(t, arm).start()
@@ -329,90 +329,104 @@
         for e in range(2):
             pack_copy(0, arm, e).wait_recv()
         forward_copy(arm).start()
+        if arm == 0:
+            send_packed(1, 1)
+    for arm in range(2):
         pass_labels(1, arm)
-    gather_round1()
     swap[1].wait_recv()
 
     for arm in range(2):
+        @pl.loop(0, 2)
+        def _(e):
+            goal, _ = ring_target(2, arm, e)
+            part[2 * arm + e] = own_sums(goal, 0)
+
+        if arm == 0:
+            gather_round1()
+            for k in range(2):
+                pass_labels(2, k)
+
+        @pl.loop(0, 2)
+        def _(e):
+            goal, _ = ring_target(2, arm, e)
+            move[2 * arm + e] = moves(arm, goal)
+
         for e in range(2):
             pack_copy(1, arm, e).wait_recv()
         forward_copy(arm).wait_recv()
-        pass_labels(2, arm)
-
-    @pl.loop(0, 4)
-    def _(q):
-        arm, e = q % 2, q // 2
-        goal, nearest = ring_target(2, arm, e)
-        part[...] = own_sums(goal, 0)
-        ring[arm, e, 0] = (part[...] + spread(arm, goal)).astype(BF16)
-        ring_copy(2, arm, e, nearest).start()
-
-    gather_round2()
+
+        @pl.loop(0, 2)
+        def _(e):
+            _, nearest = ring_target(2, arm, e)
+            come = jnp.dot(move[2 * arm + e], far[arm], preferred_element_type=F32)
+            ring[arm, e, 0] = (part[2 * arm + e] + come).astype(BF16)
+            ring_copy(2, arm, e, nearest).start()
+
+    gather_round1b()
+    for arm in range(2):
+        pass_labels(3, arm)
 
     @pl.loop(3, long_arm)
     def _(t):
         @pl.loop(0, 4)
         def _(q):
-            arm, e = q % 2, q // 2
+            arm, e = q // 2, q % 2
 
             @pl.when(t + arm < long_arm)
             def _():
                 goal, nearest = ring_target(t, arm, e)
-                part[...] = own_sums(goal, 0)
+                part[0] = own_sums(goal, 0)
                 ring_copy(t - 1, arm, e, nearest).wait_recv()
-                ring[arm, e, t - 2] = (part[...] + ring[arm, e, t - 2].astype(F32)).astype(BF16)
+                ring[arm, e, t - 2] = (part[0] + ring[arm, e, t - 2].astype(F32)).astype(BF16)
                 ring_copy(t, arm, e, nearest).start()
 
         for arm in range(2):
-            @pl.when(t + arm < long_arm)
+            @pl.when(t + arm + 1 < long_arm)
             def _():
-                pass_labels(t, arm)
+                pass_labels(t + 1, arm)
 
         @pl.when(t == 3)
         def _():
+            gather_round2()
+
+        @pl.when(t == 4)
+        def _():
             gather_round3()
 
-        @pl.when(t == 4)
+        @pl.when(t == 5)
         def _():
             gather_round4()
             take_candidates()
-
-        @pl.when(t == 5)
-        def _():
             scores()
-            softmax()
 
         @pl.when(t == 6)
         def _():
+            softmax()
             grads()
-            grad_out.start()
 
     lab_copy(long_arm - 1, 0).wait_recv()
     count(labs.at[0, long_arm])
     lab_copy(long_arm - 2, 1).wait_recv()
     count(labs.at[1, long_arm - 1])
     counts = jnp.sum(hits[...], axis=1, keepdims=True)
-    inverse = 1.0 / jnp.maximum(counts, 1.0)
+    keep = jnp.where(counts > 0, KEEP, 1.0)
+    take = jnp.where(counts > 0, (1.0 - KEEP) / jnp.maximum(counts, 1.0), 0.0)
     swap[2].wait_recv()
     local[3].wait()
     local[4].wait()
+    for which in range(2):
+        part[0] = own_sums(region, which)
+        ring_copy(long_arm - 2, 1, which, sibling).wait_recv()
+        mix[which] = keep * old[which].astype(F32) + take * (part[0] + ring[1, which, long_arm - 3].astype(F32))
     square = jnp.zeros((rows, 1), F32)
     for which in range(2):
-        part[...] = own_sums(region, which)
-        for arm in range(2):
-            ring_copy(long_arm - 1 - arm, arm, which, sibling).wait_recv()
-        sums = part[...] + ring[0, which, long_arm - 2].astype(F32) + ring[1, which, long_arm - 3].astype(F32)
-        before = old[which].astype(F32)
-        mixed = jnp.where(counts > 0, KEEP * before + (1.0 - KEEP) * (sums * inverse), before)
+        ring_copy(long_arm - 1, 0, which, sibling).wait_recv()
+        mixed = mix[which] + take * ring[0, which, long_arm - 2].astype(F32)
         mix[which] = mixed
         square += jnp.sum(mixed * mixed, axis=1, keepdims=True)
     scale = lax.rsqrt(square * (1.0 / width) + 1e-06) * width ** (-0.5)
-    outs = []
     for which, cols in ((0, my_cols), (1, other_cols)):
-        new[which] = (mix[which] * scale).astype(BF16)
-        copy = pltpu.make_async_copy(new.at[which], new_hbm.at[:, cols], loc.at[7 + which])
-        copy.start()
-        outs.append(copy)
+        new[:, cols] = (mix[which] * scale).astype(BF16)
 
     for copy in swap:
         copy.wait_send()
@@ -431,19 +445,13 @@
         def _(t):
             for e in range(2):
                 ring_copy(t, arm, e, sibling).wait_send()
-    grad_out.wait()
-    for copy in outs:
-        copy.wait()
-
-
-def hand_over(grad_in, new_in, grad_out, new_out, sem):
-    crops, rows = grad_in.shape[0], new_in.shape[0]
-    piece = rows // 2
-    copies = []
-    for source, target, count in ((grad_in, grad_out, crops), (new_in, new_out, rows)):
-        for first in range(0, count, piece):
-            span = pl.ds(first, piece)
-            copies.append(pltpu.make_async_copy(source.at[span], target.at[span], sem.at[len(copies)]))
+
+
+def hand_over(grad, new, grad_out, new_out, sem):
+    copies = [
+        pltpu.make_async_copy(grad, grad_out, sem.at[0]),
+        pltpu.make_async_copy(new, new_out, sem.at[1]),
+    ]
     for copy in copies:
         copy.start()
     for copy in copies:
@@ -465,16 +473,12 @@
         smem = pl.BlockSpec(memory_space=pltpu.SMEM)
         vmem = pl.BlockSpec(memory_space=pltpu.VMEM)
         dma = pltpu.SemaphoreType.DMA
-        shapes = (
-            jax.ShapeDtypeStruct((crops, width), BF16),
-            jax.ShapeDtypeStruct((rows, width), BF16),
-        )
         packed = 2 * max(2, 2 * crops // regions)
         results = pl.pallas_call(
             functools.partial(kernel, chips, side),
-            out_shape=shapes,
+            out_shape=(pltpu.VMEM((crops, width), BF16), pltpu.VMEM((rows, width), BF16)),
             in_specs=[any_spec, any_spec, smem, smem, vmem],
-            out_specs=(any_spec, any_spec),
+            out_specs=(vmem, vmem),
             scratch_shapes=[
                 pltpu.VMEM((crops, width), BF16),
                 pltpu.VMEM((2, 2 * crops, half), BF16),
@@ -486,14 +490,13 @@
                 pltpu.VMEM((2, arm + 1, 2, 1, 2 * crops), jnp.int32),
                 pltpu.VMEM((groups, rows, width), BF16),
                 pltpu.VMEM((2, rows, half), BF16),
-                pltpu.VMEM((rows, half), F32),
+                pltpu.VMEM((4, rows, half), F32),
+                pltpu.VMEM((4, rows, 4 * packed), BF16),
                 pltpu.VMEM((rows, crops), F32),
                 pltpu.VMEM((total, width), BF16),
                 pltpu.VMEM((crops, total), F32),
                 pltpu.VMEM((crops, total), BF16),
-                pltpu.VMEM((crops, width), BF16),
                 pltpu.VMEM((2, rows, half), F32),
-                pltpu.VMEM((2, rows, half), BF16),
                 dma((2, 2, arm - 1)),
                 dma((2, 2, arm - 1)),
                 dma((2, 5)),
@@ -504,19 +507,22 @@
                 dma((3,)),
                 dma((2, 20)),
                 dma((2, 20)),
-                dma((9,)),
+                dma((6,)),
             ],
             compiler_params=pltpu.CompilerParams(
                 collective_id=0, has_side_effects=True, vmem_limit_bytes=56 << 20
             ),
         )(features, memory, requests, owners, labels)
-        pieces = 2 * (crops + rows) // rows
+        results = [pltpu.with_memory_space_constraint(r, pltpu.VMEM) for r in results]
         return pl.pallas_call(
             hand_over,
-            out_shape=shapes,
-            in_specs=[any_spec, any_spec],
+            out_shape=(
+                jax.ShapeDtypeStruct((crops, width), BF16),
+                jax.ShapeDtypeStruct((rows, width), BF16),
+            ),
+            in_specs=[vmem, vmem],
             out_specs=(any_spec, any_spec),
-            scratch_shapes=[dma((pieces,))],
+            scratch_shapes=[dma((2,))],
         )(*results)
 
     both = P(("region", "group"), None)

time: 165 us -> 98.5 us (0.60)
  Pallas kernels: 164 us -> 97.7 us
    pallas_call x2, Pallas kernels: 164 us -> 97.7 us  [the longest x1 96.4 us: on_device(): pl.pallas_call(functools.partial(kernel, chips, side), out_shape=(pltpu.V...]
where the time goes in v3:
time: 98.5 us; the launch traced here: 98.4 us
  Pallas kernels  97.7 us (99%)
    pallas_call x1, Pallas kernels, on_device(): pl.pallas_call(functools.partial(kernel, chips, side), out_shape=(pltpu.V...  96.4 us

profile of v3, /device:TPU:1, one launch (start us, length us, event | category | flops | bytes accessed | tf_op | source)
XLA Modules:
  0.0 98.4 jit_solution(10934417707542122756)
XLA Ops:
  0.6 96.4 %shard_map.68 = (bf16[384,2048]{1,0:T(8,128)(2,1)S(1)}, bf16[128,2048]{1,0:T(8,128)(2,1)S(1)}) custom-call(bf16[384,2048]{1,0:T(8,128)(2,1)} %feat_hbm.1, bf16[128,2048]{1,0:T(8,128)(2,1)} %mem_hbm.1, s32[1,8]{1,0:T(1,128)} %req_ref.1, s32[1,16]{1,0:T(1,128)} %own_ref.1, s32[1,384]{1,0:T(1,128)} %lab_ref.1), custom_call_target="tpu_custom_call" | custom-call | tf_op jit(solution)/shard_map/pallas_call | solution.py:477
  97.0 1.3 %shard_map.69 = (bf16[384,2048]{1,0:T(8,128)(2,1)}, bf16[128,2048]{1,0:T(8,128)(2,1)}) custom-call(bf16[384,2048]{1,0:T(8,128)(2,1)S(1)} %get-tuple-element.4.grad, bf16[128,2048]{1,0:T(8,128)(2,1)S(1)} %get-tuple-element.5.new), custom_call_target="tpu_custom_call" | custom-call | tf_op jit(solution)/shard_map/pallas_call | solution.py:517

commit v4 on v3

--- a/solution.py
+++ b/solution.py
@@ -18,10 +18,10 @@
 
 def kernel(
     chips, side,
-    feat_hbm, mem_hbm, req_ref, own_ref, lab_ref,
+    feat_hbm, mem_hbm, req_hbm, own_hbm, lab_hbm,
     grad, new,
-    feat, halves, ring, packs, near, far, pair, labs, gath, old, part, move, hits, cand, score, logit, mix,
-    ring_send, ring_recv, pack_send, pack_recv, lab_send, lab_recv, sib_send, sib_recv, ag_send, ag_recv, loc,
+    req_ref, own_ref, lab_ref, feat, halves, ring, packs, near, far, pair, labs, tallies, gath, old, part, move, cand, score, logit, mix,
+    ring_send, ring_recv, pack_send, pack_recv, lab_send, lab_recv, tally_send, tally_recv, sib_send, sib_recv, ag_send, ag_recv, last_send, last_recv, loc,
 ):
     crops, width = feat.shape
     half = width // 2
@@ -59,6 +59,11 @@
     for partner in partners:
         pl.semaphore_signal(barrier, inc=1, device_id=partner, device_id_type=MESH)
 
+    tables = [
+        pltpu.make_async_copy(lab_hbm, lab_ref, loc.at[6]),
+        pltpu.make_async_copy(req_hbm, req_ref, loc.at[7]),
+        pltpu.make_async_copy(own_hbm, own_ref, loc.at[8]),
+    ]
     local = [
         pltpu.make_async_copy(feat_hbm.at[:, my_cols], halves.at[0, pl.ds(0, crops)], loc.at[0]),
         pltpu.make_async_copy(feat_hbm.at[:, other_cols], halves.at[1, pl.ds(0, crops)], loc.at[1]),
@@ -67,22 +72,38 @@
         pltpu.make_async_copy(mem_hbm.at[:, other_cols], old.at[1], loc.at[4]),
         pltpu.make_async_copy(mem_hbm, gath.at[group], loc.at[5]),
     ]
-    for copy in local:
-        copy.start()
-
+    tables[0].start()
+    local[0].start()
+    local[1].start()
+
+    before_crop = jnp.where(
+        lax.broadcasted_iota(jnp.int32, (crops, crops), 0) < lax.broadcasted_iota(jnp.int32, (crops, crops), 1),
+        1.0, 0.0,
+    ).astype(BF16)
+    tables[0].wait()
     label = lab_ref[...]
     label_region = lax.shift_right_logical(label, jnp.int32(rows.bit_length() - 1))
     of_region = jnp.where(
         lax.broadcasted_iota(jnp.int32, (2 * chips, crops), 0) == label_region, 1.0, 0.0
     )
-    before_crop = jnp.where(
-        lax.broadcasted_iota(jnp.int32, (crops, crops), 0) < lax.broadcasted_iota(jnp.int32, (crops, crops), 1),
-        1.0, 0.0,
-    ).astype(BF16)
     earlier = jnp.dot(of_region.astype(BF16), before_crop, preferred_element_type=F32)
     rank = jnp.sum(earlier * of_region, axis=0, keepdims=True).astype(jnp.int32)
-    pair[0, :, 0:crops] = label
-    pair[0, :, crops:2 * crops] = label_region * slots + rank
+    slot_row = label_region * slots + rank
+    lanes = pair.shape[2]
+    pieces = crops // lanes
+    pair[0] = jnp.zeros(pair.shape[1:], jnp.int32)
+    for n in range(pieces):
+        pair[0, n:n + 1, :] = label[:, n * lanes:(n + 1) * lanes]
+        pair[0, pieces + n:pieces + n + 1, :] = slot_row[:, n * lanes:(n + 1) * lanes]
+
+    def row_of(tiles, k, first):
+        return jnp.concatenate([tiles[k, first + n:first + n + 1, :] for n in range(pieces)], axis=1)
+
+    def labels_of(tiles, k):
+        return row_of(tiles, k, 0)
+
+    def slots_of(tiles, k):
+        return row_of(tiles, k, pieces)
 
     pl.semaphore_wait(barrier, len(partners))
 
@@ -98,6 +119,24 @@
         remote(feat_hbm.at[:, my_cols], halves.at[1, pl.ds(crops, crops)], sib_send.at[2], sib_recv.at[2], sibling),
     ]
     swap[0].start()
+
+    def tile_copy(arm, e):
+        towards = sign * (1 - 2 * arm) * (1 - 2 * e)
+        return remote(
+            pair.at[0], labs.at[arm, 0, e], lab_send.at[arm, e], lab_recv.at[arm, e],
+            dev(chip_at(towards), core + e * sign, group),
+        )
+
+    def tiles_copy(arm):
+        towards = sign * (1 - 2 * arm)
+        return remote(
+            labs.at[arm, 0], labs.at[arm, 1], lab_send.at[arm, 2], lab_recv.at[arm, 2],
+            dev(chip_at(towards), core, group),
+        )
+
+    for arm in range(2):
+        for e in range(2):
+            tile_copy(arm, e).start()
 
     def pack_copy(stage, arm, e):
         towards = sign * (1 - 2 * arm) * (1 - 2 * e)
@@ -122,7 +161,7 @@
             towards = sign * (1 - 2 * arm) * (1 - 2 * e)
             goal = chip_at(towards * (long_arm - arm - stage))
             take = jnp.where(
-                lax.broadcasted_iota(jnp.int32, (packed, crops), 0) + goal * packed == pair[0, :, crops:2 * crops],
+                lax.broadcasted_iota(jnp.int32, (packed, crops), 0) + goal * packed == slots_of(pair, 0),
                 1.0, 0.0,
             ).astype(BF16)
             packs[stage, arm, e] = jnp.dot(
@@ -133,6 +172,12 @@
     local[0].wait()
     local[1].wait()
     send_packed(0, 0)
+    swap[1].start()
+    send_packed(1, 0)
+    send_packed(0, 1)
+    swap[2].start()
+    for copy in local[2:] + tables[1:]:
+        copy.start()
 
     offs = (0, -1, 1, 2)
 
@@ -227,42 +272,50 @@
                     q2(h, a, u).wait_send()
 
     gather_round0()
-    send_packed(1, 0)
-    swap[1].start()
-    swap[2].start()
-    send_packed(0, 1)
 
     places = lax.broadcasted_iota(jnp.int32, (rows, crops), 0)
 
     def hit(label_row, target):
         return jnp.where(places == label_row - target * rows, 1.0, 0.0)
 
-    def own_sums(target, which):
-        pick = jnp.concatenate([hit(pair[k, :, 0:crops], target) for k in range(2)], axis=1).astype(BF16)
+    def own_pick(target):
+        return jnp.concatenate([hit(labels_of(pair, k), target) for k in range(2)], axis=1).astype(BF16)
+
+    def own_sums(pick, which):
         return jnp.dot(pick, halves[which], preferred_element_type=F32)
 
-    def count(label_pair):
-        hits[...] += hit(label_pair[0, :, 0:crops], region) + hit(label_pair[1, :, 0:crops], region)
+    def tally(pick):
+        ones = jnp.ones((tallies.shape[2], pick.shape[1]), BF16)
+        return lax.dot_general(ones, pick, (((1,), (1,)), ((), ())), preferred_element_type=F32)
 
     def moves(arm, target):
-        sources = [(labs.at[arm, hop], k) for hop in (1, 2) for k in range(2)]
+        sources = [(labs.at[arm, hop], k) for hop in range(2) for k in range(2)]
         first = target // 2 * packed
         put, take = [], []
         for n, (source, k) in enumerate(sources):
-            slot = source[k, :, crops:2 * crops] - first
+            slot = slots_of(source, k) - first
             slot = jnp.where((slot >= 0) & (slot < packed), slot + n * packed, -1)
             place = lax.broadcasted_iota(jnp.int32, (4 * packed, crops), 0)
             take.append(jnp.where(place == slot, 1.0, 0.0).astype(BF16))
-            put.append(hit(source[k, :, 0:crops], target).astype(BF16))
-        return lax.dot_general(
-            jnp.concatenate(put, axis=1), jnp.concatenate(take, axis=1), (((1,), (1,)), ((), ())),
-            preferred_element_type=F32,
-        ).astype(BF16)
+            put.append(hit(labels_of(source, k), target).astype(BF16))
+        put = jnp.concatenate(put, axis=1)
+        through = lax.dot_general(
+            put, jnp.concatenate(take, axis=1), (((1,), (1,)), ((), ())), preferred_element_type=F32
+        )
+        return through.astype(BF16), tally(put)
 
     def ring_copy(t, arm, e, device):
         return remote(
             ring.at[arm, e, t - 2], ring.at[arm, e, t - 1], ring_send.at[arm, e, t - 2], ring_recv.at[arm, e, t - 1],
             device,
+        )
+
+    def last_copy(e, r):
+        span = pl.ds(r * (rows // 2), rows // 2)
+        _, nearest = ring_target(long_arm - 1, 0, e)
+        return remote(
+            ring.at[0, e, long_arm - 3, span], ring.at[0, e, long_arm - 2, span], last_send.at[e, r], last_recv.at[e, r],
+            nearest,
         )
 
     def ring_target(t, arm, e):
@@ -273,21 +326,22 @@
         nearest = dev(chip_at(towards), core + last * e * sign, group)
         return goal, nearest
 
-    def lab_copy(t, arm):
+    def tally_copy(t, arm):
         towards = sign * (1 - 2 * arm)
         return remote(
-            labs.at[arm, t], labs.at[arm, t + 1], lab_send.at[arm, t], lab_recv.at[arm, t + 1],
+            tallies.at[arm, t - 2], tallies.at[arm, t - 1], tally_send.at[arm, t - 2], tally_recv.at[arm, t - 1],
             dev(chip_at(towards), core, group),
         )
 
+    for arm in range(2):
+        for e in range(2):
+            tile_copy(arm, e).wait_recv()
+        tiles_copy(arm).start()
     swap[0].wait_recv()
-    for arm in range(2):
-        labs[arm, 0] = pair[...]
-        lab_copy(0, arm).start()
-    hits[...] = jnp.zeros_like(hits)
-    count(pair)
 
     def take_candidates():
+        tables[1].wait()
+        tables[2].wait()
         for k in range(8):
             cand[k * rows:(k + 1) * rows, :] = gath[own_ref[0, req_ref[0, k]]]
 
@@ -320,36 +374,34 @@
             span = pl.ds(pl.multiple_of(n * 256, 256), 256)
             grad[:, span] = jnp.dot(logit[...], cand[:, span], preferred_element_type=F32).astype(BF16)
 
-    def pass_labels(t, arm):
-        lab_copy(t - 1, arm).wait_recv()
-        lab_copy(t, arm).start()
-        count(labs.at[arm, t])
-
     for arm in range(2):
         for e in range(2):
             pack_copy(0, arm, e).wait_recv()
         forward_copy(arm).start()
         if arm == 0:
             send_packed(1, 1)
-    for arm in range(2):
-        pass_labels(1, arm)
     swap[1].wait_recv()
 
     for arm in range(2):
         @pl.loop(0, 2)
         def _(e):
             goal, _ = ring_target(2, arm, e)
-            part[2 * arm + e] = own_sums(goal, 0)
+            part[2 * arm + e] = own_sums(own_pick(goal), 0)
 
         if arm == 0:
             gather_round1()
-            for k in range(2):
-                pass_labels(2, k)
+        tiles_copy(arm).wait_recv()
 
         @pl.loop(0, 2)
         def _(e):
             goal, _ = ring_target(2, arm, e)
-            move[2 * arm + e] = moves(arm, goal)
+            through, number = moves(arm, goal)
+            move[2 * arm + e] = through
+
+            @pl.when(e == 0)
+            def _():
+                tallies[arm, 0] = number + tally(own_pick(goal))
+                tally_copy(2, arm).start()
 
         for e in range(2):
             pack_copy(1, arm, e).wait_recv()
@@ -363,27 +415,26 @@
             ring_copy(2, arm, e, nearest).start()
 
     gather_round1b()
-    for arm in range(2):
-        pass_labels(3, arm)
-
-    @pl.loop(3, long_arm)
+
+    @pl.loop(3, long_arm - 1)
     def _(t):
         @pl.loop(0, 4)
         def _(q):
             arm, e = q // 2, q % 2
-
-            @pl.when(t + arm < long_arm)
+            goal, nearest = ring_target(t, arm, e)
+            pick = own_pick(goal)
+            part[0] = own_sums(pick, 0)
+
+            @pl.when(e == 0)
             def _():
-                goal, nearest = ring_target(t, arm, e)
-                part[0] = own_sums(goal, 0)
-                ring_copy(t - 1, arm, e, nearest).wait_recv()
-                ring[arm, e, t - 2] = (part[0] + ring[arm, e, t - 2].astype(F32)).astype(BF16)
-                ring_copy(t, arm, e, nearest).start()
-
-        for arm in range(2):
-            @pl.when(t + arm + 1 < long_arm)
-            def _():
-                pass_labels(t + 1, arm)
+                number = tally(pick)
+                tally_copy(t - 1, arm).wait_recv()
+                tallies[arm, t - 2] = tallies[arm, t - 2] + number
+                tally_copy(t, arm).start()
+
+            ring_copy(t - 1, arm, e, nearest).wait_recv()
+            ring[arm, e, t - 2] = (part[0] + ring[arm, e, t - 2].astype(F32)).astype(BF16)
+            ring_copy(t, arm, e, nearest).start()
 
         @pl.when(t == 3)
         def _():
@@ -404,29 +455,55 @@
             softmax()
             grads()
 
-    lab_copy(long_arm - 1, 0).wait_recv()
-    count(labs.at[0, long_arm])
-    lab_copy(long_arm - 2, 1).wait_recv()
-    count(labs.at[1, long_arm - 1])
-    counts = jnp.sum(hits[...], axis=1, keepdims=True)
+    for e in range(2):
+        goal, _ = ring_target(long_arm - 1, 0, e)
+        pick = own_pick(goal)
+        part[0] = own_sums(pick, 0)
+        if e == 0:
+            number = tally(pick)
+            tally_copy(long_arm - 2, 0).wait_recv()
+            tallies[0, long_arm - 3] = tallies[0, long_arm - 3] + number
+            tally_copy(long_arm - 1, 0).start()
+        ring_copy(long_arm - 2, 0, e, sibling).wait_recv()
+        for r in range(2):
+            span = pl.ds(r * (rows // 2), rows // 2)
+            ring[0, e, long_arm - 3, span, :] = (
+                part[0, span, :] + ring[0, e, long_arm - 3, span, :].astype(F32)
+            ).astype(BF16)
+            last_copy(e, r).start()
+
+    pick = own_pick(region)
+    tally_copy(long_arm - 2, 1).wait_recv()
+    tally_copy(long_arm - 1, 0).wait_recv()
+    number = tally(pick) + tallies[0, long_arm - 2] + tallies[1, long_arm - 3]
+    square_of = (rows, rows)
+    diagonal = lax.broadcasted_iota(jnp.int32, square_of, 0) == lax.broadcasted_iota(jnp.int32, square_of, 1)
+    counts = jnp.sum(jnp.where(diagonal, number[0:1, :], 0.0), axis=1, keepdims=True)
     keep = jnp.where(counts > 0, KEEP, 1.0)
     take = jnp.where(counts > 0, (1.0 - KEEP) / jnp.maximum(counts, 1.0), 0.0)
     swap[2].wait_recv()
     local[3].wait()
     local[4].wait()
     for which in range(2):
-        part[0] = own_sums(region, which)
+        part[0] = own_sums(pick, which)
         ring_copy(long_arm - 2, 1, which, sibling).wait_recv()
         mix[which] = keep * old[which].astype(F32) + take * (part[0] + ring[1, which, long_arm - 3].astype(F32))
-    square = jnp.zeros((rows, 1), F32)
-    for which in range(2):
-        ring_copy(long_arm - 1, 0, which, sibling).wait_recv()
-        mixed = mix[which] + take * ring[0, which, long_arm - 2].astype(F32)
-        mix[which] = mixed
-        square += jnp.sum(mixed * mixed, axis=1, keepdims=True)
-    scale = lax.rsqrt(square * (1.0 / width) + 1e-06) * width ** (-0.5)
+    square = [None, None]
     for which, cols in ((0, my_cols), (1, other_cols)):
-        new[:, cols] = (mix[which] * scale).astype(BF16)
+        for r in range(2):
+            span = pl.ds(r * (rows // 2), rows // 2)
+            last_copy(which, r).wait_recv()
+            mixed = mix[which, span, :] + take[r * (rows // 2):(r + 1) * (rows // 2)] * ring[
+                0, which, long_arm - 2, span, :
+            ].astype(F32)
+            ones = jnp.sum(mixed * mixed, axis=1, keepdims=True)
+            if which == 0:
+                mix[0, span, :] = mixed
+                square[r] = ones
+            else:
+                scale = lax.rsqrt((square[r] + ones) * (1.0 / width) + 1e-06) * width ** (-0.5)
+                new[span, cols] = (mixed * scale).astype(BF16)
+                new[span, my_cols] = (mix[0, span, :] * scale).astype(BF16)
 
     for copy in swap:
         copy.wait_send()
@@ -437,14 +514,19 @@
             for stage in range(2):
                 pack_copy(stage, arm, e).wait_send()
 
-        @pl.loop(0, long_arm - arm)
+        tiles_copy(arm).wait_send()
+        for e in range(2):
+            tile_copy(arm, e).wait_send()
+
+        @pl.loop(2, long_arm - 1)
         def _(t):
-            lab_copy(t, arm).wait_send()
-
-        @pl.loop(2, long_arm - arm)
-        def _(t):
+            tally_copy(t, arm).wait_send()
             for e in range(2):
                 ring_copy(t, arm, e, sibling).wait_send()
+    tally_copy(long_arm - 1, 0).wait_send()
+    for e in range(2):
+        for r in range(2):
+            last_copy(e, r).wait_send()
 
 
 def hand_over(grad, new, grad_out, new_out, sem):
@@ -470,29 +552,31 @@
         arm = chips // 2
         total = requests.shape[1] * rows
         any_spec = pl.BlockSpec(memory_space=pl.ANY)
-        smem = pl.BlockSpec(memory_space=pltpu.SMEM)
         vmem = pl.BlockSpec(memory_space=pltpu.VMEM)
         dma = pltpu.SemaphoreType.DMA
         packed = 2 * max(2, 2 * crops // regions)
         results = pl.pallas_call(
             functools.partial(kernel, chips, side),
             out_shape=(pltpu.VMEM((crops, width), BF16), pltpu.VMEM((rows, width), BF16)),
-            in_specs=[any_spec, any_spec, smem, smem, vmem],
+            in_specs=[any_spec] * 5,
             out_specs=(vmem, vmem),
             scratch_shapes=[
+                pltpu.SMEM(requests.shape, jnp.int32),
+                pltpu.SMEM(owners.shape, jnp.int32),
+                pltpu.VMEM(labels.shape, jnp.int32),
                 pltpu.VMEM((crops, width), BF16),
                 pltpu.VMEM((2, 2 * crops, half), BF16),
                 pltpu.VMEM((2, 2, arm - 1, rows, half), BF16),
                 pltpu.VMEM((2, 2, 2, packed, half), BF16),
                 pltpu.VMEM((2, 2 * packed, half), BF16),
                 pltpu.VMEM((2, 4 * packed, half), BF16),
-                pltpu.VMEM((2, 1, 2 * crops), jnp.int32),
-                pltpu.VMEM((2, arm + 1, 2, 1, 2 * crops), jnp.int32),
+                pltpu.VMEM((2, 8, 128), jnp.int32),
+                pltpu.VMEM((2, 2, 2, 8, 128), jnp.int32),
+                pltpu.VMEM((2, arm - 1, 8, 128), F32),
                 pltpu.VMEM((groups, rows, width), BF16),
                 pltpu.VMEM((2, rows, half), BF16),
                 pltpu.VMEM((4, rows, half), F32),
                 pltpu.VMEM((4, rows, 4 * packed), BF16),
-                pltpu.VMEM((rows, crops), F32),
                 pltpu.VMEM((total, width), BF16),
                 pltpu.VMEM((crops, total), F32),
                 pltpu.VMEM((crops, total), BF16),
@@ -501,13 +585,17 @@
                 dma((2, 2, arm - 1)),
                 dma((2, 5)),
                 dma((2, 5)),
-                dma((2, arm + 1)),
-                dma((2, arm + 1)),
+                dma((2, 3)),
+                dma((2, 3)),
+                dma((2, arm - 1)),
+                dma((2, arm - 1)),
                 dma((3,)),
                 dma((3,)),
                 dma((2, 20)),
                 dma((2, 20)),
-                dma((6,)),
+                dma((2, 2)),
+                dma((2, 2)),
+                dma((9,)),
             ],
             compiler_params=pltpu.CompilerParams(
                 collective_id=0, has_side_effects=True, vmem_limit_bytes=56 << 20

time: 98.5 us -> 95.3 us (0.968)
  Pallas kernels: 97.7 us -> 94.5 us
    pallas_call x1, Pallas kernels: 96.4 us -> 93.2 us  [on_device(): pl.pallas_call(functools.partial(kernel, chips, side), out_shape=(pltpu.V...]
where the time goes in v4:
time: 95.3 us; the launch traced here: 95.2 us
  Pallas kernels  94.5 us (99%)
    pallas_call x1, Pallas kernels, on_device(): pl.pallas_call(functools.partial(kernel, chips, side), out_shape=(pltpu.V...  93.2 us

profile of v4, /device:TPU:1, one launch (start us, length us, event | category | flops | bytes accessed | tf_op | source)
XLA Modules:
  0.0 95.2 jit_solution(16477810652424081446)
XLA Ops:
  0.6 93.2 %shard_map.68 = (bf16[384,2048]{1,0:T(8,128)(2,1)S(1)}, bf16[128,2048]{1,0:T(8,128)(2,1)S(1)}) custom-call(bf16[384,2048]{1,0:T(8,128)(2,1)} %feat_hbm.1, bf16[128,2048]{1,0:T(8,128)(2,1)} %mem_hbm.1, s32[1,8]{1,0:T(1,128)} %req_hbm.1, s32[1,16]{1,0:T(1,128)} %own_hbm.1, s32[1,384]{1,0:T(1,128)} %lab_hbm.1), custom_call_target="tpu_custom_call" | custom-call | tf_op jit(solution)/shard_map/pallas_call | solution.py:558
  93.8 1.3 %shard_map.69 = (bf16[384,2048]{1,0:T(8,128)(2,1)}, bf16[128,2048]{1,0:T(8,128)(2,1)}) custom-call(bf16[384,2048]{1,0:T(8,128)(2,1)S(1)} %get-tuple-element.4.grad, bf16[128,2048]{1,0:T(8,128)(2,1)S(1)} %get-tuple-element.5.new), custom_call_target="tpu_custom_call" | custom-call | tf_op jit(solution)/shard_map/pallas_call | solution.py:605

commit v5 on v4

--- a/solution.py
+++ b/solution.py
@@ -21,7 +21,7 @@
     feat_hbm, mem_hbm, req_hbm, own_hbm, lab_hbm,
     grad, new,
     req_ref, own_ref, lab_ref, feat, halves, ring, packs, near, far, pair, labs, tallies, gath, old, part, move, cand, score, logit, mix,
-    ring_send, ring_recv, pack_send, pack_recv, lab_send, lab_recv, tally_send, tally_recv, sib_send, sib_recv, ag_send, ag_recv, last_send, last_recv, loc,
+    ring_send, ring_recv, pack_send, pack_recv, lab_send, lab_recv, tally_send, tally_recv, sib_send, sib_recv, ag_send, ag_recv, last_recv, loc,
 ):
     crops, width = feat.shape
     half = width // 2
@@ -76,25 +76,29 @@
     local[0].start()
     local[1].start()
 
-    before_crop = jnp.where(
-        lax.broadcasted_iota(jnp.int32, (crops, crops), 0) < lax.broadcasted_iota(jnp.int32, (crops, crops), 1),
-        1.0, 0.0,
-    ).astype(BF16)
-    tables[0].wait()
-    label = lab_ref[...]
-    label_region = lax.shift_right_logical(label, jnp.int32(rows.bit_length() - 1))
-    of_region = jnp.where(
-        lax.broadcasted_iota(jnp.int32, (2 * chips, crops), 0) == label_region, 1.0, 0.0
-    )
-    earlier = jnp.dot(of_region.astype(BF16), before_crop, preferred_element_type=F32)
-    rank = jnp.sum(earlier * of_region, axis=0, keepdims=True).astype(jnp.int32)
-    slot_row = label_region * slots + rank
     lanes = pair.shape[2]
     pieces = crops // lanes
+    square_of = (lanes, lanes)
+    sooner = jnp.where(
+        lax.broadcasted_iota(jnp.int32, square_of, 0) < lax.broadcasted_iota(jnp.int32, square_of, 1), 1.0, 0.0
+    ).astype(BF16)
     pair[0] = jnp.zeros(pair.shape[1:], jnp.int32)
+    region_of = lax.broadcasted_iota(jnp.int32, (2 * chips, lanes), 0)
+    tables[0].wait()
+    split = [lab_ref[:, n * lanes:(n + 1) * lanes] for n in range(pieces)]
+    homes = [lax.shift_right_logical(piece, jnp.int32(rows.bit_length() - 1)) for piece in split]
+    of_region = [jnp.where(region_of == home, 1.0, 0.0) for home in homes]
+    earlier = jnp.dot(
+        jnp.concatenate(of_region, axis=0).astype(BF16), sooner, preferred_element_type=F32
+    )
+    seen = jnp.zeros((2 * chips, 1), F32)
     for n in range(pieces):
-        pair[0, n:n + 1, :] = label[:, n * lanes:(n + 1) * lanes]
-        pair[0, pieces + n:pieces + n + 1, :] = slot_row[:, n * lanes:(n + 1) * lanes]
+        rank = jnp.sum(
+            (earlier[n * 2 * chips:(n + 1) * 2 * chips] + seen) * of_region[n], axis=0, keepdims=True
+        ).astype(jnp.int32)
+        seen += jnp.sum(of_region[n], axis=1, keepdims=True)
+        pair[0, n:n + 1, :] = split[n]
+        pair[0, pieces + n:pieces + n + 1, :] = homes[n] * slots + rank
 
     def row_of(tiles, k, first):
         return jnp.concatenate([tiles[k, first + n:first + n + 1, :] for n in range(pieces)], axis=1)
@@ -116,21 +120,21 @@
     swap = [
         remote(pair.at[0], pair.at[1], sib_send.at[0], sib_recv.at[0], sibling),
         remote(feat_hbm.at[:, other_cols], halves.at[0, pl.ds(crops, crops)], sib_send.at[1], sib_recv.at[1], sibling),
-        remote(feat_hbm.at[:, my_cols], halves.at[1, pl.ds(crops, crops)], sib_send.at[2], sib_recv.at[2], sibling),
+        remote(feat_hbm.at[:, my_cols], halves.at[1, pl.ds(crops, crops)], sib_send.at[1], sib_recv.at[2], sibling),
     ]
     swap[0].start()
 
     def tile_copy(arm, e):
         towards = sign * (1 - 2 * arm) * (1 - 2 * e)
         return remote(
-            pair.at[0], labs.at[arm, 0, e], lab_send.at[arm, e], lab_recv.at[arm, e],
+            pair.at[0], labs.at[arm, 0, e], lab_send.at[0], lab_recv.at[arm, 0],
             dev(chip_at(towards), core + e * sign, group),
         )
 
     def tiles_copy(arm):
         towards = sign * (1 - 2 * arm)
         return remote(
-            labs.at[arm, 0], labs.at[arm, 1], lab_send.at[arm, 2], lab_recv.at[arm, 2],
+            labs.at[arm, 0], labs.at[arm, 1], lab_send.at[0], lab_recv.at[arm, 1],
             dev(chip_at(towards), core, group),
         )
 
@@ -144,16 +148,20 @@
         landing = near if stage == 0 else far
         return remote(
             packs.at[stage, arm, e], landing.at[arm, place],
-            pack_send.at[arm, 2 * stage + e], pack_recv.at[arm, 2 * stage + e],
+            pack_send.at[0], pack_recv.at[arm, stage],
             dev(chip_at(towards), core + e * sign, group),
         )
 
     def forward_copy(arm):
         towards = sign * (1 - 2 * arm)
         return remote(
-            near.at[arm], far.at[arm, pl.ds(2 * packed, 2 * packed)], pack_send.at[arm, 4], pack_recv.at[arm, 4],
+            near.at[arm], far.at[arm, pl.ds(2 * packed, 2 * packed)], pack_send.at[1], pack_recv.at[arm, 1],
             dev(chip_at(towards), core, group),
         )
+
+    def packs_here(arm, stage):
+        landing = (near if stage == 0 else far).at[arm]
+        return remote(landing, landing, pack_send.at[0], pack_recv.at[arm, stage], sibling)
 
     def send_packed(stage, arm):
         @pl.loop(0, 2)
@@ -187,30 +195,29 @@
         dx, dy = (i, j) if h == 0 else (j, i)
         return at_xy(dx, dy)
 
-    def ag_copy(h, index, src_block, rows_of, device_block, own=False):
+    def ag_copy(h, kind, src_block, rows_of, device_block, own=False):
         cols = pl.ds(h * half, half)
         dst = gath.at[src_block, rows_of, cols]
         src = mem_hbm.at[rows_of, cols] if own else dst
-        return remote(src, dst, ag_send.at[h, index], ag_recv.at[h, index], (region, device_block))
+        return remote(src, dst, ag_send.at[kind], ag_recv.at[kind], (region, device_block))
 
     full = pl.ds(0, rows)
     part_of = {1: pl.ds(0, rows // 2), -1: pl.ds(rows // 2, rows // 2)}
-    way = {1: 0, -1: 1}
 
     def p1(h, u, recv=False):
-        return ag_copy(h, way[u], block(h, -u, 0) if recv else block(h, 0, 0), full, block(h, u, 0), own=not recv)
+        return ag_copy(h, 0, block(h, -u, 0) if recv else block(h, 0, 0), full, block(h, u, 0), own=not recv)
 
     def p2(h, u, recv=False):
-        return ag_copy(h, 2 + way[u], block(h, -2 * u if recv else -u, 0), part_of[u], block(h, u, 0))
+        return ag_copy(h, 1, block(h, -2 * u if recv else -u, 0), part_of[u], block(h, u, 0))
 
     def q1(h, a, u, recv=False):
         return ag_copy(
-            h, 4 + 2 * a + way[u], block(h, offs[a], -u if recv else 0), full, block(h, 0, u), own=(a == 0 and not recv)
+            h, (2, 3, 3, 4)[a], block(h, offs[a], -u if recv else 0), full, block(h, 0, u), own=(a == 0 and not recv)
         )
 
     def q2(h, a, u, recv=False):
         return ag_copy(
-            h, 12 + 2 * a + way[u], block(h, offs[a], -2 * u if recv else -u), part_of[u], block(h, 0, u)
+            h, 5, block(h, offs[a], -2 * u if recv else -u), part_of[u], block(h, 0, u)
         )
 
     both = (1, -1)
@@ -223,53 +230,50 @@
             for h in range(2):
                 q1(h, 0, u).start()
 
+    amounts = (2, 1, 2, 4, 2, 4)
+
+    def whole(kind):
+        some = gath.at[pl.ds(0, amounts[kind])]
+        return remote(some, some, ag_send.at[kind], ag_recv.at[kind], sibling)
+
     def gather_round1():
+        whole(0).wait_recv()
         for h in range(2):
             for u, a in ((1, 1), (-1, 2)):
-                p1(h, u, True).wait_recv()
                 p2(h, u).start()
                 for v in both:
                     q1(h, a, v).start()
 
     def gather_round1b():
+        whole(2).wait_recv()
         for h in range(2):
             for u in both:
-                q1(h, 0, u, True).wait_recv()
                 q2(h, 0, u).start()
 
     def gather_round2():
+        whole(1).wait_recv()
         for h in range(2):
             for u in both:
-                p2(h, u, True).wait_recv()
-            for u in both:
                 q1(h, 3, u).start()
+        whole(3).wait_recv()
         for h in range(2):
             for a in (1, 2):
                 for u in both:
-                    q1(h, a, u, True).wait_recv()
                     q2(h, a, u).start()
 
     def gather_round3():
+        whole(4).wait_recv()
         for h in range(2):
             for u in both:
-                q1(h, 3, u, True).wait_recv()
                 q2(h, 3, u).start()
 
     def gather_round4():
-        for h in range(2):
-            for a in range(4):
-                for u in both:
-                    q2(h, a, u, True).wait_recv()
+        whole(5).wait_recv()
         local[5].wait()
 
     def gather_sent():
-        for h in range(2):
-            for u in both:
-                p1(h, u).wait_send()
-                p2(h, u).wait_send()
-                for a in range(4):
-                    q1(h, a, u).wait_send()
-                    q2(h, a, u).wait_send()
+        for kind in range(len(amounts)):
+            whole(kind).wait_send()
 
     gather_round0()
 
@@ -306,7 +310,7 @@
 
     def ring_copy(t, arm, e, device):
         return remote(
-            ring.at[arm, e, t - 2], ring.at[arm, e, t - 1], ring_send.at[arm, e, t - 2], ring_recv.at[arm, e, t - 1],
+            ring.at[arm, e, t - 2], ring.at[arm, e, t - 1], ring_send.at[arm], ring_recv.at[arm, e, t - 2],
             device,
         )
 
@@ -314,7 +318,7 @@
         span = pl.ds(r * (rows // 2), rows // 2)
         _, nearest = ring_target(long_arm - 1, 0, e)
         return remote(
-            ring.at[0, e, long_arm - 3, span], ring.at[0, e, long_arm - 2, span], last_send.at[e, r], last_recv.at[e, r],
+            ring.at[0, e, long_arm - 3, span], ring.at[0, e, long_arm - 2, span], ring_send.at[0], last_recv.at[e, r],
             nearest,
         )
 
@@ -329,13 +333,12 @@
     def tally_copy(t, arm):
         towards = sign * (1 - 2 * arm)
         return remote(
-            tallies.at[arm, t - 2], tallies.at[arm, t - 1], tally_send.at[arm, t - 2], tally_recv.at[arm, t - 1],
+            tallies.at[arm, t - 2], tallies.at[arm, t - 1], tally_send.at[arm], tally_recv.at[arm, t - 2],
             dev(chip_at(towards), core, group),
         )
 
     for arm in range(2):
-        for e in range(2):
-            tile_copy(arm, e).wait_recv()
+        remote(pair, labs.at[arm, 0], lab_send.at[0], lab_recv.at[arm, 0], sibling).wait_recv()
         tiles_copy(arm).start()
     swap[0].wait_recv()
 
@@ -375,8 +378,7 @@
             grad[:, span] = jnp.dot(logit[...], cand[:, span], preferred_element_type=F32).astype(BF16)
 
     for arm in range(2):
-        for e in range(2):
-            pack_copy(0, arm, e).wait_recv()
+        packs_here(arm, 0).wait_recv()
         forward_copy(arm).start()
         if arm == 0:
             send_packed(1, 1)
@@ -403,9 +405,7 @@
                 tallies[arm, 0] = number + tally(own_pick(goal))
                 tally_copy(2, arm).start()
 
-        for e in range(2):
-            pack_copy(1, arm, e).wait_recv()
-        forward_copy(arm).wait_recv()
+        packs_here(arm, 1).wait_recv()
 
         @pl.loop(0, 2)
         def _(e):
@@ -476,8 +476,8 @@
     tally_copy(long_arm - 2, 1).wait_recv()
     tally_copy(long_arm - 1, 0).wait_recv()
     number = tally(pick) + tallies[0, long_arm - 2] + tallies[1, long_arm - 3]
-    square_of = (rows, rows)
-    diagonal = lax.broadcasted_iota(jnp.int32, square_of, 0) == lax.broadcasted_iota(jnp.int32, square_of, 1)
+    own_place = (rows, rows)
+    diagonal = lax.broadcasted_iota(jnp.int32, own_place, 0) == lax.broadcasted_iota(jnp.int32, own_place, 1)
     counts = jnp.sum(jnp.where(diagonal, number[0:1, :], 0.0), axis=1, keepdims=True)
     keep = jnp.where(counts > 0, KEEP, 1.0)
     take = jnp.where(counts > 0, (1.0 - KEEP) / jnp.maximum(counts, 1.0), 0.0)
@@ -488,6 +488,12 @@
         part[0] = own_sums(pick, which)
         ring_copy(long_arm - 2, 1, which, sibling).wait_recv()
         mix[which] = keep * old[which].astype(F32) + take * (part[0] + ring[1, which, long_arm - 3].astype(F32))
+    swap[0].wait_send()
+    remote(halves.at[0], halves.at[0], sib_send.at[1], sib_recv.at[1], sibling).wait_send()
+    gather_sent()
+    remote(packs, packs, pack_send.at[0], pack_recv.at[0, 0], sibling).wait_send()
+    remote(near, near, pack_send.at[1], pack_recv.at[0, 0], sibling).wait_send()
+    remote(labs, labs, lab_send.at[0], lab_recv.at[0, 0], sibling).wait_send()
     square = [None, None]
     for which, cols in ((0, my_cols), (1, other_cols)):
         for r in range(2):
@@ -505,28 +511,11 @@
                 new[span, cols] = (mixed * scale).astype(BF16)
                 new[span, my_cols] = (mix[0, span, :] * scale).astype(BF16)
 
-    for copy in swap:
-        copy.wait_send()
-    gather_sent()
     for arm in range(2):
-        forward_copy(arm).wait_send()
-        for e in range(2):
-            for stage in range(2):
-                pack_copy(stage, arm, e).wait_send()
-
-        tiles_copy(arm).wait_send()
-        for e in range(2):
-            tile_copy(arm, e).wait_send()
-
-        @pl.loop(2, long_arm - 1)
-        def _(t):
-            tally_copy(t, arm).wait_send()
-            for e in range(2):
-                ring_copy(t, arm, e, sibling).wait_send()
-    tally_copy(long_arm - 1, 0).wait_send()
-    for e in range(2):
-        for r in range(2):
-            last_copy(e, r).wait_send()
+        sent = tallies.at[arm, pl.ds(0, long_arm - 2 - arm)]
+        remote(sent, sent, tally_send.at[arm], tally_recv.at[arm, 0], sibling).wait_send()
+        sent = ring.at[arm, :, pl.ds(0, long_arm - 2 - arm)]
+        remote(sent, sent, ring_send.at[arm], ring_recv.at[arm, 0, 0], sibling).wait_send()
 
 
 def hand_over(grad, new, grad_out, new_out, sem):
@@ -581,19 +570,18 @@
                 pltpu.VMEM((crops, total), F32),
                 pltpu.VMEM((crops, total), BF16),
                 pltpu.VMEM((2, rows, half), F32),
-                dma((2, 2, arm - 1)),
-                dma((2, 2, arm - 1)),
-                dma((2, 5)),
-                dma((2, 5)),
-                dma((2, 3)),
-                dma((2, 3)),
-                dma((2, arm - 1)),
-                dma((2, arm - 1)),
+                dma((2,)),
+                dma((2, 2, arm - 3)),
+                dma((2,)),
+                dma((2, 2)),
+                dma((1,)),
+                dma((2, 2)),
+                dma((2,)),
+                dma((2, arm - 2)),
+                dma((2,)),
                 dma((3,)),
-                dma((3,)),
-                dma((2, 20)),
-                dma((2, 20)),
-                dma((2, 2)),
+                dma((6,)),
+                dma((6,)),
                 dma((2, 2)),
                 dma((9,)),
             ],

time: 95.3 us -> 93.8 us (0.984)
  Pallas kernels: 94.5 us -> 93.1 us
    pallas_call x1, Pallas kernels: 93.2 us -> 91.7 us  [on_device(): pl.pallas_call(functools.partial(kernel, chips, side), out_shape=(pltpu.V...]
where the time goes in v5:
time: 93.8 us; the launch traced here: 93.7 us
  Pallas kernels  93.1 us (99%)
    pallas_call x1, Pallas kernels, on_device(): pl.pallas_call(functools.partial(kernel, chips, side), out_shape=(pltpu.V...  91.7 us

profile of v5, /device:TPU:1, one launch (start us, length us, event | category | flops | bytes accessed | tf_op | source)
XLA Modules:
  0.0 93.7 jit_solution(12209265731982171499)
XLA Ops:
  0.6 91.7 %shard_map.68 = (bf16[384,2048]{1,0:T(8,128)(2,1)S(1)}, bf16[128,2048]{1,0:T(8,128)(2,1)S(1)}) custom-call(bf16[384,2048]{1,0:T(8,128)(2,1)} %feat_hbm.1, bf16[128,2048]{1,0:T(8,128)(2,1)} %mem_hbm.1, s32[1,8]{1,0:T(1,128)} %req_hbm.1, s32[1,16]{1,0:T(1,128)} %own_hbm.1, s32[1,384]{1,0:T(1,128)} %lab_hbm.1), custom_call_target="tpu_custom_call" | custom-call | tf_op jit(solution)/shard_map/pallas_call | solution.py:547
  92.4 1.3 %shard_map.69 = (bf16[384,2048]{1,0:T(8,128)(2,1)}, bf16[128,2048]{1,0:T(8,128)(2,1)}) custom-call(bf16[384,2048]{1,0:T(8,128)(2,1)S(1)} %get-tuple-element.4.grad, bf16[128,2048]{1,0:T(8,128)(2,1)S(1)} %get-tuple-element.5.new), custom_call_target="tpu_custom_call" | custom-call | tf_op jit(solution)/shard_map/pallas_call | solution.py:593

commit v6 on v5

--- a/solution.py
+++ b/solution.py
@@ -289,8 +289,8 @@
         return jnp.dot(pick, halves[which], preferred_element_type=F32)
 
     def tally(pick):
-        ones = jnp.ones((tallies.shape[2], pick.shape[1]), BF16)
-        return lax.dot_general(ones, pick, (((1,), (1,)), ((), ())), preferred_element_type=F32)
+        ones = jnp.ones((8, pick.shape[1]), BF16)
+        return lax.dot_general(ones, pick, (((1,), (1,)), ((), ())), preferred_element_type=F32)[0:1]
 
     def moves(arm, target):
         sources = [(labs.at[arm, hop], k) for hop in range(2) for k in range(2)]
@@ -478,7 +478,7 @@
     number = tally(pick) + tallies[0, long_arm - 2] + tallies[1, long_arm - 3]
     own_place = (rows, rows)
     diagonal = lax.broadcasted_iota(jnp.int32, own_place, 0) == lax.broadcasted_iota(jnp.int32, own_place, 1)
-    counts = jnp.sum(jnp.where(diagonal, number[0:1, :], 0.0), axis=1, keepdims=True)
+    counts = jnp.sum(jnp.where(diagonal, number, 0.0), axis=1, keepdims=True)
     keep = jnp.where(counts > 0, KEEP, 1.0)
     take = jnp.where(counts > 0, (1.0 - KEEP) / jnp.maximum(counts, 1.0), 0.0)
     swap[2].wait_recv()
@@ -561,7 +561,7 @@
                 pltpu.VMEM((2, 4 * packed, half), BF16),
                 pltpu.VMEM((2, 8, 128), jnp.int32),
                 pltpu.VMEM((2, 2, 2, 8, 128), jnp.int32),
-                pltpu.VMEM((2, arm - 1, 8, 128), F32),
+                pltpu.VMEM((2, arm - 1, 1, rows), F32),
                 pltpu.VMEM((groups, rows, width), BF16),
                 pltpu.VMEM((2, rows, half), BF16),
                 pltpu.VMEM((4, rows, half), F32),

time: 93.8 us -> 93.5 us (level)
  no operation moved by 1% of the time
where the time goes in v6:
time: 93.5 us; the launch traced here: 93.4 us
  Pallas kernels  92.7 us (99%)
    pallas_call x1, Pallas kernels, on_device(): pl.pallas_call(functools.partial(kernel, chips, side), out_shape=(pltpu.V...  91.4 us

profile of v6, /device:TPU:1, one launch (start us, length us, event | category | flops | bytes accessed | tf_op | source)
XLA Modules:
  0.0 93.4 jit_solution(8441044027572489341)
XLA Ops:
  0.6 91.4 %shard_map.68 = (bf16[384,2048]{1,0:T(8,128)(2,1)S(1)}, bf16[128,2048]{1,0:T(8,128)(2,1)S(1)}) custom-call(bf16[384,2048]{1,0:T(8,128)(2,1)} %feat_hbm.1, bf16[128,2048]{1,0:T(8,128)(2,1)} %mem_hbm.1, s32[1,8]{1,0:T(1,128)} %req_hbm.1, s32[1,16]{1,0:T(1,128)} %own_hbm.1, s32[1,384]{1,0:T(1,128)} %lab_hbm.1), custom_call_target="tpu_custom_call" | custom-call | tf_op jit(solution)/shard_map/pallas_call | solution.py:547
  92.1 1.3 %shard_map.69 = (bf16[384,2048]{1,0:T(8,128)(2,1)}, bf16[128,2048]{1,0:T(8,128)(2,1)}) custom-call(bf16[384,2048]{1,0:T(8,128)(2,1)S(1)} %get-tuple-element.4.grad, bf16[128,2048]{1,0:T(8,128)(2,1)S(1)} %get-tuple-element.5.new), custom_call_target="tpu_custom_call" | custom-call | tf_op jit(solution)/shard_map/pallas_call | solution.py:593
